TPU v7x, 512 devices: a whole 4x4x16 slice. The times are simulated.
512 devices in a mesh: dp: 32 (over z, core), expert: 16 (over x, y).
Axes of the slice: x: 4, y: 4, z: 16, core: 2. Of those that a mesh axis runs over, the one named last changes fastest.
Arguments:
- tokens: bfloat16 [5120, 4096], P('expert', 'dp'), may hold values from -6 to 6
- out_grad: bfloat16 [5120, 4096], P('expert', 'dp'), may hold values from -0.29882812 to 0.29882812
- slot_tokens: int32 [4, 160], replicated, may hold values from 0 to 5119, as said below
- slot_gate: float32 [4, 160], replicated, may hold values from 0.1 to 1
- w_gate: bfloat16 [16, 4096, 2048], P('expert', 'dp'), may hold values from -0.09375 to 0.09375
- w_up: bfloat16 [16, 4096, 2048], P('expert', 'dp'), may hold values from -0.09375 to 0.09375
- w_down: bfloat16 [16, 2048, 4096], P('expert', None, 'dp'), may hold values from -0.0625 to 0.0625
Outputs:
- grad_tokens: bfloat16 [5120, 4096], P('expert', 'dp')
- grad_w_gate: bfloat16 [16, 4096, 2048], P('expert', 'dp')
- grad_w_up: bfloat16 [16, 4096, 2048], P('expert', 'dp')
- grad_w_down: bfloat16 [16, 2048, 4096], P('expert', None, 'dp')
- grad_gates: float32 [16, 40], P('expert')
Inputs may be any that keep to these rules, and one draw needn't show every extreme that they name: `slot_tokens`: row e lists 160 distinct token numbers, ordered by their owner t // 320 ascending. At most 20 of a row come from the 320 tokens of one owner, and in every row exactly 20 come from one owner.
All inputs are finite; a program needn't handle non-finite values.
Results may differ from a plain program's by a relative error of at most 0.0057.
Values may be sent and summed in bfloat16 or wider, within the bound.
No kernel may reach another device: no remote copies, remote signals or barrier semaphores. Data moves between devices by JAX's collectives and lax.ppermute only.
A program may use at most 64 MiB of HBM per device.

v0:
```python
import jax
import jax.numpy as jnp
from jax import lax
from jax.sharding import PartitionSpec as P

GROUP = 4


def partner(value, axis, distance):
    mask = 2**distance
    pairs = [(source, source ^ mask) for source in range(lax.axis_size(axis))]
    return lax.ppermute(value, axis, pairs)


def contract_rows(left, right):
    return lax.dot_general(
        left, right, (((0,), (0,)), ((), ())), preferred_element_type=jnp.float32
    )


def contract_cols(left, right):
    return lax.dot_general(
        left, right, (((1,), (1,)), ((), ())), preferred_element_type=jnp.float32
    )


def slot_ranking(owners, owner_count):
    owner_range = jnp.arange(owner_count, dtype=jnp.int32)
    onehot = (owners[:, :, None] == owner_range[None, None, :]).astype(jnp.int32)
    before = jnp.cumsum(onehot, axis=1) - onehot
    return jnp.sum(before * onehot, axis=2)


def gated_grads(upstream, pre_gate, pre_up, sigmoid_gate):
    gate_side = (upstream * pre_up * sigmoid_gate * (1.0 + pre_gate * (1.0 - sigmoid_gate))).astype(
        jnp.bfloat16
    )
    up_side = (upstream * pre_gate * sigmoid_gate).astype(jnp.bfloat16)
    return (gate_side, up_side)


def per_device(tokens, out_grad, slot_tokens, slot_gate, w_gate, w_up, w_down):
    owner_count = lax.axis_size("expert")
    position = lax.axis_index("expert")
    token_rows = tokens.shape[0]
    feature_cols = tokens.shape[1]
    flight_count, capacity = slot_tokens.shape
    bucket_size = GROUP * max(1, capacity // (2 * owner_count))
    owners = slot_tokens // token_rows
    slot_rank = slot_ranking(owners, owner_count)
    is_mine = owners == position
    local_index = slot_tokens - position * token_rows
    expert_rows = jnp.broadcast_to(
        jnp.arange(flight_count, dtype=jnp.int32)[:, None], (flight_count, capacity)
    )
    column_index = jnp.where(is_mine, slot_rank, bucket_size)
    send_table = (
        jnp.zeros((flight_count, bucket_size + 1), jnp.int32)
        .at[expert_rows, column_index]
        .set(local_index)[:, :bucket_size]
    )
    filled = (
        jnp.zeros((flight_count, bucket_size + 1), jnp.int32)
        .at[expert_rows, column_index]
        .set(1)[:, :bucket_size]
    )
    send_index = jnp.repeat(send_table, GROUP, axis=0)
    send_valid = jnp.repeat(filled, GROUP, axis=0) > 0
    input_send = jnp.where(send_valid[:, :, None], tokens[send_index], jnp.zeros((), jnp.bfloat16))
    grad_send = jnp.where(send_valid[:, :, None], out_grad[send_index], jnp.zeros((), jnp.bfloat16))
    input_recv, grad_recv = (
        lax.all_to_all(input_send, "expert", split_axis=0, concat_axis=0, tiled=True),
        lax.all_to_all(grad_send, "expert", split_axis=0, concat_axis=0, tiled=True),
    )
    expert_here = position // GROUP
    quarter = position % GROUP
    owner_here = lax.dynamic_index_in_dim(owners, expert_here, 0, keepdims=False)
    rank_here = lax.dynamic_index_in_dim(slot_rank, expert_here, 0, keepdims=False)
    bucket_flat = owner_here * bucket_size + rank_here
    slot_inputs = input_recv.reshape(owner_count * bucket_size, feature_cols)[bucket_flat]
    slot_grads = grad_recv.reshape(owner_count * bucket_size, feature_cols)[bucket_flat]
    gates_here = lax.dynamic_index_in_dim(slot_gate, expert_here, 0, keepdims=False)
    gate_weight = w_gate[0]
    up_weight = w_up[0]
    down_weight = w_down[0]
    part_gate = jnp.dot(slot_inputs, gate_weight, preferred_element_type=jnp.float32)
    part_up = jnp.dot(slot_inputs, up_weight, preferred_element_type=jnp.float32)
    pre_gate, pre_up = lax.psum((part_gate, part_up), "dp")
    sigmoid_gate = jax.nn.sigmoid(pre_gate)
    hidden = (pre_gate * sigmoid_gate * pre_up).astype(jnp.bfloat16)
    local_out = jnp.dot(hidden, down_weight, preferred_element_type=jnp.float32)
    gate_part = jnp.sum(slot_grads.astype(jnp.float32) * local_out, axis=1)
    scaled = (gates_here[:, None] * slot_grads.astype(jnp.float32)).astype(jnp.bfloat16)
    grad_down = contract_rows(hidden, scaled).astype(jnp.bfloat16)
    part_hidden = contract_cols(scaled, down_weight)
    grad_hidden = lax.psum(part_hidden, "dp")
    gate_side, up_side = gated_grads(grad_hidden, pre_gate, pre_up, sigmoid_gate)
    gate_total = lax.psum(gate_part, "dp")
    grad_gate_weight = contract_rows(slot_inputs, gate_side).astype(jnp.bfloat16)
    grad_up_weight = contract_rows(slot_inputs, up_side).astype(jnp.bfloat16)
    slot_back = contract_cols(gate_side, gate_weight) + contract_cols(up_side, up_weight)
    for bit_number in range(GROUP.bit_length() - 1):
        gate_total = gate_total + partner(gate_total, "expert", bit_number)
    outgoing = (
        jnp.zeros((owner_count * bucket_size, feature_cols), jnp.float32)
        .at[bucket_flat]
        .set(slot_back)
    )
    incoming = lax.all_to_all(
        outgoing.reshape(owner_count, bucket_size, feature_cols),
        "expert",
        split_axis=0,
        concat_axis=0,
        tiled=True,
    )
    target = jnp.where(send_valid, send_index, token_rows)
    summed = (
        jnp.zeros((token_rows + 1, feature_cols), jnp.float32)
        .at[target.reshape(-1)]
        .add(incoming.reshape(-1, feature_cols))
    )
    grad_tokens = summed[:token_rows].astype(jnp.bfloat16)
    gate_width = capacity // GROUP
    grad_gates = lax.dynamic_slice_in_dim(gate_total, quarter * gate_width, gate_width)[None, :]
    return (grad_tokens, grad_gate_weight[None], grad_up_weight[None], grad_down[None], grad_gates)


def solution(mesh):
    in_specs = (
        P("expert", "dp"),
        P("expert", "dp"),
        P(),
        P(),
        P("expert", "dp", None),
        P("expert", "dp", None),
        P("expert", None, "dp"),
    )
    out_specs = (
        P("expert", "dp"),
        P("expert", "dp", None),
        P("expert", "dp", None),
        P("expert", None, "dp"),
        P("expert", None),
    )
    return jax.shard_map(
        per_device, mesh=mesh, in_specs=in_specs, out_specs=out_specs, check_vma=False
    )
```

profile of v0, /device:TPU:1, one launch (start us, length us, event | category | flops | bytes accessed | tf_op | source)
XLA Modules:
  0.0 408.8 jit_solution(8496324978233504566)
XLA Ops:
  7.2 0.8 broadcast_subtract_fusion
  8.1 2.3 reduce-window.6
  10.8 29.9 %scatter_fusion = s32[4,21]{1,0:T(4,128)S(1)} fusion(s32[4,21]{1,0:T(4,128)S(1)} %broadcast.144.clone.1, s32[640]{0:T(1024)S(1)} %reshape.195, s32[640]{0:T(1024)S(1)} %broadcast.189), kind=kCustom, calls=%fused_computation.4 | custom fusion | bytes 12800 | tf_op jit(solution)/shard_map/scatter | solution.py:65
  40.7 29.9 %scatter_fusion.1 = s32[4,21]{1,0:T(4,128)S(1)} fusion(s32[4,21]{1,0:T(4,128)S(1)} %broadcast.144.clone, s32[640]{0:T(1024)S(1)} %reshape.195, s32[640]{0:T(1024)S(1)} %reshape.203), kind=kCustom, calls=%fused_computation.5 | custom fusion | bytes 12800 | tf_op jit(solution)/shard_map/scatter | solution.py:60
  70.7 1.4 gather_fusion.2
  72.2 1.4 gather_fusion
  73.6 0.8 broadcast_select_fusion.1
  74.4 7.6 %all-to-all-start = ((bf16[16,20,128]{2,1,0:T(8,128)(2,1)}), bf16[16,20,128]{2,1,0:T(8,128)(2,1)S(1)}, u32[]{:S(2)}, u32[]{:S(2)}) async-start(bf16[16,20,128]{2,1,0:T(8,128)(2,1)} %get-tuple-element.13), calls=%async_computation | async-start | bytes 196608 | tf_op jit(solution)/shard_map/all_to_all | solution.py:73
  82.1 6.5 %all-to-all-done = bf16[16,20,128]{2,1,0:T(8,128)(2,1)S(1)} async-done(((bf16[16,20,128]{2,1,0:T(8,128)(2,1)}), bf16[16,20,128]{2,1,0:T(8,128)(2,1)S(1)}, u32[]{:S(2)}, u32[]{:S(2)}) %all-to-all-start) | async-done | bytes 81952 | tf_op jit(solution)/shard_map/all_to_all | solution.py:73
  88.6 3.5 all-to-all-start.1
  92.2 0.7 constant_dynamic-slice_fusion
  92.9 0.8 gather_fusion.1
  93.7 5.0 %all-to-all-done.1 = bf16[16,20,128]{2,1,0:T(8,128)(2,1)S(1)} async-done(((bf16[16,20,128]{2,1,0:T(8,128)(2,1)}), bf16[16,20,128]{2,1,0:T(8,128)(2,1)S(1)}, u32[]{:S(2)}, u32[]{:S(2)}) %all-to-all-start.1) | async-done | bytes 81952 | tf_op jit(solution)/shard_map/all_to_all | solution.py:72
  98.7 0.8 gather_fusion.3
  99.5 1.4 fusion.6
  100.9 1.4 fusion.9
  102.3 1.5 fusion.12
  103.9 224.8 %all-reduce.4.cloned.1.call-done = (f32[160,2048]{1,0:T(8,128)}, f32[160,2048]{1,0:T(8,128)}, f32[160,2048]{1,0:T(8,128)}) async-done(((f32[160,2048]{1,0:T(8,128)}, f32[160,2048]{1,0:T(8,128)}, f32[160,2048]{1,0:T(8,128)}), (f32[160,2048]{1,0:T(8,128)}, f32[160,2048]{1,0:T(8,128)}, f32[160,2048]{1,0:T(8,128)})) %all-reduce.4.cloned.1.call-update) | async-done | bytes 3932176 | tf_op jit(solution)/shard_map/psum | solution.py:88
  328.7 3.0 multiply_convert_fusion
  331.7 0.4 fusion.3
  332.1 1.3 fusion.2
  333.5 45.9 %psum.31 = f32[160]{0:T(256)S(1)} all-reduce(f32[160]{0:T(256)S(1)} %fusion.3), channel_id=1, replica_groups=mesh['dp'=32,'expert'=16] {'dp'}, use_global_device_ids=true, to_apply=%region_11.12 | all-reduce | flops 160 | bytes 1280 | tf_op jit(solution)/shard_map/psum | solution.py:98
  379.4 3.1 collective-permute-start
  383.2 1.1 fusion
  384.3 1.0 scatter_custom_fusion.2
  385.3 0.7 reshape.160
  386.0 6.2 %all-to-all-start.2 = ((f32[16,20,128]{2,1,0:T(8,128)}), f32[16,20,128]{2,1,0:T(8,128)S(1)}, u32[]{:S(2)}, u32[]{:S(2)}) async-start(f32[16,20,128]{2,1,0:T(8,128)} %reshape.160), calls=%async_computation.2 | async-start | bytes 393216 | tf_op jit(solution)/shard_map/all_to_all | solution.py:109
  392.3 4.8 %collective-permute-start.1 = (f32[160]{0:T(256)S(1)}, f32[160]{0:T(256)S(1)}, u32[]{:S(2)}, u32[]{:S(2)}) collective-permute-start(f32[160]{0:T(256)S(1)} %add.108), channel_id=1, source_target_pairs={{0,2},{1,3},{2,0},{3,1},{4,6},{5,7},{6,4},{7,5},{8,10},{9,11},{10,... | collective-permute-start | bytes 1928 | tf_op jit(solution)/shard_map/ppermute | solution.py:12
  397.1 1.1 fusion.1
  398.2 0.6 dynamic-slice_bitcast_fusion
  399.2 2.1 scatter_custom_fusion.3
  401.3 0.6 slice.48
  (50 shorter events, 2.1 us)
Async XLA Ops:
  7.2 92.3 %copy-start = (bf16[1,128,2048]{2,1,0:T(8,128)(2,1)S(1)}, bf16[1,128,2048]{2,1,0:T(8,128)(2,1)}, u32[]{:S(2)}) copy-start(bf16[1,128,2048]{2,1,0:T(8,128)(2,1)} %param.11) | copy-start | bytes 1572868
  40.7 30.0 %copy-start.1 = (bf16[320,128]{1,0:T(8,128)(2,1)S(1)}, bf16[320,128]{1,0:T(8,128)(2,1)}, u32[]{:S(2)}) copy-start(bf16[320,128]{1,0:T(8,128)(2,1)} %param.7) | copy-start | bytes 245764
  70.6 1.6 copy-start.2
  74.4 14.2 %all-to-all-start = ((bf16[16,20,128]{2,1,0:T(8,128)(2,1)}), bf16[16,20,128]{2,1,0:T(8,128)(2,1)S(1)}, u32[]{:S(2)}, u32[]{:S(2)}) async-start(bf16[16,20,128]{2,1,0:T(8,128)(2,1)} %get-tuple-element.13), calls=%async_computation | async-start | bytes 196608 | tf_op jit(solution)/shard_map/all_to_all | solution.py:73
  88.6 10.1 %all-to-all-start.1 = ((bf16[16,20,128]{2,1,0:T(8,128)(2,1)}), bf16[16,20,128]{2,1,0:T(8,128)(2,1)S(1)}, u32[]{:S(2)}, u32[]{:S(2)}) async-start(bf16[16,20,128]{2,1,0:T(8,128)(2,1)} %get-tuple-element.14), calls=%async_computation.1 | async-start | bytes 196608 | tf_op jit(solution)/shard_map/all_to_all | solution.py:72
  92.1 236.6 %all-reduce.4.cloned.1.call-start = ((), (), s32[]{:S(2)}) async-start(), calls=%async_computation.3 | async-start | bytes 7864320 | tf_op jit(solution)/shard_map/psum | solution.py:88
  92.9 8.0 %copy-start.4 = (bf16[1,128,2048]{2,1,0:T(8,128)(2,1)S(1)}, bf16[1,128,2048]{2,1,0:T(8,128)(2,1)}, u32[]{:S(2)}) copy-start(bf16[1,128,2048]{2,1,0:T(8,128)(2,1)} %param.12) | copy-start | bytes 1572868
  100.9 1.4 copy-start.3
  379.4 12.9 %collective-permute-start = (f32[160]{0:T(256)S(1)}, f32[160]{0:T(256)S(1)}, u32[]{:S(2)}, u32[]{:S(2)}) collective-permute-start(f32[160]{0:T(256)S(1)} %psum.31), channel_id=1, source_target_pairs={{0,1},{1,0},{2,3},{3,2},{4,5},{5,4},{6,7},{7,6},{8,9},{9,8},{10,11... | collective-permute-start | bytes 1928 | tf_op jit(solution)/shard_map/ppermute | solution.py:12
  386.0 13.2 %all-to-all-start.2 = ((f32[16,20,128]{2,1,0:T(8,128)}), f32[16,20,128]{2,1,0:T(8,128)S(1)}, u32[]{:S(2)}, u32[]{:S(2)}) async-start(f32[16,20,128]{2,1,0:T(8,128)} %reshape.160), calls=%async_computation.2 | async-start | bytes 393216 | tf_op jit(solution)/shard_map/all_to_all | solution.py:109
  392.3 5.9 %collective-permute-start.1 = (f32[160]{0:T(256)S(1)}, f32[160]{0:T(256)S(1)}, u32[]{:S(2)}, u32[]{:S(2)}) collective-permute-start(f32[160]{0:T(256)S(1)} %add.108), channel_id=1, source_target_pairs={{0,2},{1,3},{2,0},{3,1},{4,6},{5,7},{6,4},{7,5},{8,10},{9,11},{10,... | collective-permute-start | bytes 1928 | tf_op jit(solution)/shard_map/ppermute | solution.py:12
Sparse Core Ops, SparseCore 0:
  103.9 224.7 all-reduce.3
where the time goes:
time: 413 us; the launch traced here: 409 us
  waiting for transfers between devices  237 us (57%)
  local copies, waits for them, and re-layouts  68.4 us (17%)
  blocking collectives  45.9 us (11%)
  starting transfers between devices  25.2 us (6%)
  between operations  14.4 us (3%)
  other arithmetic  9.11 us (2%)
  matrix products  8.99 us (2%)
    psum x1, waiting for transfers between devices, per_device(): pre_gate, pre_up = lax.psum((part_gate, part_up), 'dp')  225 us
    psum x1, blocking collectives, per_device(): gate_total = lax.psum(gate_part, 'dp')  45.9 us
    scatter x1, local copies, waits for them, and re-layouts, per_device(): send_table = jnp.zeros((flight_count, bucket_size + 1), jnp.int32).at[exp...  29.9 us
    scatter x1, local copies, waits for them, and re-layouts, per_device(): filled = jnp.zeros((flight_count, bucket_size + 1), jnp.int32).at[expert_...  29.9 us
  transfers between devices with their start and end apart: 6, of which 4 were waited for; matrix products, arithmetic and copies ran while one was open for 2% of the time, Pallas kernels for 0%

commit v1 on v0

v1 whole, which is shorter than its diff:
```python
import jax
import jax.numpy as jnp
import numpy as np
from jax import lax
from jax.experimental import pallas as pl
from jax.experimental.pallas import tpu as pltpu
from jax.sharding import Mesh
from jax.sharding import PartitionSpec as P

BF16 = jnp.bfloat16
F32 = jnp.float32
I32 = jnp.int32

TOK = 320
CAP = 160
HALF = 80
OWNERS = 16
FLIGHT = 4
ROOM = 24
LANES = 128
BLOCKS = 16
PIECE = 3 * HALF + 8

VMEM = pl.BlockSpec(memory_space=pltpu.VMEM)


def iota(shape, dim):
    return lax.broadcasted_iota(I32, shape, dim)


def dot(left, right, left_dim=1, right_dim=0, precision=None):
    return lax.dot_general(
        left,
        right,
        (((left_dim,), (right_dim,)), ((), ())),
        preferred_element_type=F32,
        precision=precision,
    )


def owned_tokens(row, first, rows):
    start = jnp.sum((row < first).astype(I32), axis=1, keepdims=True)
    count = jnp.sum(((row >= first) & (row < first + TOK)).astype(I32), axis=1, keepdims=True)
    rank = lax.rem(iota((rows, CAP), 0), ROOM)
    chosen = (iota((rows, CAP), 1) == start + rank) & (rank < count)
    token = jnp.sum(jnp.where(chosen, row - first + 1, 0), axis=1, keepdims=True)
    return token - 1


def column(row, core):
    slot = lax.rem(iota((CAP, CAP), 0) + HALF * core, CAP)
    return jnp.sum(jnp.where(iota((CAP, CAP), 1) == slot, row, 0), axis=1, keepdims=True)


def places(row, core):
    token = column(row, core)
    owner = jnp.sum(
        ((iota((CAP, LANES), 1) < OWNERS - 1) & (token >= TOK * (iota((CAP, LANES), 1) + 1))).astype(I32),
        axis=1,
        keepdims=True,
    )
    start = jnp.sum((row < TOK * owner).astype(I32), axis=1, keepdims=True)
    slot = lax.rem(iota((CAP, 1), 0) + HALF * core, CAP)
    return owner, slot - start


def dispatch_kernel(slots_ref, tokens_ref, grads_ref, send_ref):
    first = TOK * (4 * lax.axis_index("x") + lax.axis_index("y"))
    rows = 2 * ROOM
    for expert in range(FLIGHT):
        local = owned_tokens(slots_ref[expert : expert + 1, :], first, rows)
        hit = local == iota((rows, TOK), 1)
        upper = iota((rows, TOK), 0) < ROOM
        pick_tokens = jnp.where(hit & upper, 1.0, 0.0).astype(BF16)
        pick_grads = jnp.where(hit & ~upper, 1.0, 0.0).astype(BF16)
        rows_out = (dot(pick_tokens, tokens_ref[...]) + dot(pick_grads, grads_ref[...])).astype(BF16)
        for part in range(4):
            send_ref[4 * expert + part] = rows_out


def front_kernel(
    slots_ref, gates_ref, recv_ref, gate_ref, up_ref, down_ref, keep_ref, send_ref, inputs_ref, scaled_ref
):
    expert = lax.axis_index("x")
    core = lax.axis_index("core")
    row = slots_ref[pl.ds(expert, 1), :]
    owner, rank = places(row, core)
    place = owner * (2 * ROOM) + rank
    width = OWNERS * 2 * ROOM
    recv = recv_ref[...].reshape(width, LANES)
    where = iota((CAP, width), 1)
    inputs = dot(jnp.where(where == place, 1.0, 0.0).astype(BF16), recv).astype(BF16)
    grads = dot(jnp.where(where == place + ROOM, 1.0, 0.0).astype(BF16), recv)
    gates = column(gates_ref[pl.ds(expert, 1), :], core)
    scaled = (gates * grads).astype(BF16)
    inputs_ref[...] = inputs
    scaled_ref[...] = scaled
    for pair in range(BLOCKS // 2):
        cols = slice(256 * pair, 256 * pair + 256)
        sums = (
            dot(inputs, gate_ref[:, cols]),
            dot(inputs, up_ref[:, cols]),
            dot(scaled, down_ref[cols, :], 1, 1),
        )
        for which, total in enumerate(sums):
            for side in range(2):
                lanes = slice(LANES * side, LANES * side + LANES)
                rows = slice(HALF * which, HALF * which + HALF)
                keep_ref[2 * pair + side, rows, :] = total[:HALF, lanes]
                send_ref[2 * pair + side, rows, :] = total[HALF:, lanes]


def middle_kernel(gates_ref, parts_ref, out_ref):
    core = lax.axis_index("core")
    gates = column(gates_ref[pl.ds(lax.axis_index("x"), 1), :], core)[:HALF]

    def total(which):
        rows = slice(HALF * which, HALF * which + HALF)
        result = parts_ref[0, rows, :].astype(F32)
        for block in range(1, BLOCKS):
            result = result + parts_ref[block, rows, :].astype(F32)
        return result

    pre_gate, pre_up, upstream = total(0), total(1), total(2)
    sigmoid = jax.nn.sigmoid(pre_gate)
    hidden = (pre_gate * sigmoid * pre_up).astype(BF16)
    out_ref[:HALF, :] = hidden
    out_ref[HALF : 2 * HALF, :] = (upstream * pre_up * sigmoid * (1.0 + pre_gate * (1.0 - sigmoid))).astype(BF16)
    out_ref[2 * HALF : 3 * HALF, :] = (upstream * pre_gate * sigmoid).astype(BF16)
    part = jnp.sum(hidden.astype(F32) * upstream, axis=1, keepdims=True) / gates
    eye = iota((HALF, LANES), 0) == iota((HALF, LANES), 1)
    part = jnp.sum(jnp.where(eye, part, 0.0), axis=0, keepdims=True)
    high = part.astype(BF16).astype(F32)
    line = iota((8, LANES), 0)
    tail = jnp.where(line == 0, high, jnp.where(line == 1, part - high, 0.0))
    out_ref[3 * HALF :, :] = tail.astype(BF16)


def back_kernel(
    slots_ref,
    inputs_ref,
    scaled_ref,
    mine_ref,
    other_ref,
    gate_ref,
    up_ref,
    grad_gate_ref,
    grad_up_ref,
    grad_down_ref,
    send_ref,
):
    core = lax.axis_index("core")
    inputs = inputs_ref[...]
    scaled = scaled_ref[...]

    def joined(which, pair):
        rows = slice(HALF * which, HALF * which + HALF)
        sides = [
            jnp.concatenate([mine_ref[block, rows, :], other_ref[block, rows, :]], axis=0)
            for block in (2 * pair, 2 * pair + 1)
        ]
        return jnp.concatenate(sides, axis=1)

    back = jnp.zeros((CAP, LANES), F32)
    for pair in range(BLOCKS // 2):
        cols = slice(256 * pair, 256 * pair + 256)
        hidden, gate_side, up_side = joined(0, pair), joined(1, pair), joined(2, pair)
        grad_gate_ref[:, cols] = dot(inputs, gate_side, 0, 0).astype(BF16)
        grad_up_ref[:, cols] = dot(inputs, up_side, 0, 0).astype(BF16)
        grad_down_ref[cols, :] = dot(hidden, scaled, 0, 0).astype(BF16)
        back = back + dot(gate_side, gate_ref[:, cols], 1, 1) + dot(up_side, up_ref[:, cols], 1, 1)

    row = slots_ref[pl.ds(lax.axis_index("x"), 1), :]
    owner, rank = places(row, core)
    spread = jnp.where(iota((CAP, OWNERS * ROOM), 1) == owner * ROOM + rank, 1.0, 0.0)
    buckets = dot(spread, back, 0, 0, lax.Precision.HIGHEST).reshape(OWNERS, ROOM, LANES)

    def gate_row(ref):
        lines = jnp.zeros((8, LANES), F32)
        for block in range(BLOCKS):
            lines = lines + ref[block, 3 * HALF :, :].astype(F32)
        return jnp.broadcast_to(jnp.sum(lines, axis=0, keepdims=True), (8, LANES))

    gates_mine, gates_other = gate_row(mine_ref), gate_row(other_ref)
    line = iota((8, LANES), 0)
    for quarter in range(4):
        slot = iota((LANES, LANES), 1) + 40 * quarter
        place = lax.rem(slot + HALF * core, CAP)
        source = iota((LANES, LANES), 0)
        valid = iota((LANES, LANES), 1) < 40
        take_mine = jnp.where(valid & (place < HALF) & (source == place), 1.0, 0.0)
        take_other = jnp.where(valid & (place >= HALF) & (source == place - HALF), 1.0, 0.0)
        gates = dot(gates_mine, take_mine, precision=lax.Precision.HIGHEST) + dot(
            gates_other, take_other, precision=lax.Precision.HIGHEST
        )
        for expert in range(FLIGHT):
            bucket = buckets[4 * expert + quarter]
            send_ref[4 * expert + quarter, :16, :] = bucket[:16]
            send_ref[4 * expert + quarter, 16:, :] = jnp.where(line == 4, gates, bucket[16:])


def last_kernel(slots_ref, incoming_ref, tokens_ref, gates_ref):
    expert_here = lax.axis_index("x")
    first = TOK * (4 * expert_here + lax.axis_index("y"))
    total = jnp.zeros((TOK, LANES), F32)
    for expert in range(FLIGHT):
        local = owned_tokens(slots_ref[expert : expert + 1, :], first, ROOM)
        pick = jnp.where(local == iota((ROOM, TOK), 1), 1.0, 0.0)
        rows = incoming_ref[4 * expert]
        for part in range(1, 4):
            rows = rows + incoming_ref[4 * expert + part]
        total = total + dot(pick, rows, 0, 0, lax.Precision.HIGHEST)
    tokens_ref[...] = total.astype(BF16)
    gates = incoming_ref[4 * expert_here, 16:, :]
    for part in range(1, 4):
        gates = gates + incoming_ref[4 * expert_here + part, 16:, :]
    gates_ref[...] = gates[4:5, :]


def call(kernel, out_shape, inputs):
    return pl.pallas_call(
        kernel,
        out_shape=out_shape,
        in_specs=[VMEM] * len(inputs),
        out_specs=jax.tree.map(lambda _: VMEM, out_shape),
    )(*inputs)


def shape(dims, kind):
    return jax.ShapeDtypeStruct(dims, kind)


def swap_cores(value):
    return lax.ppermute(value, "core", [(0, 1), (1, 0)])


def per_device(tokens, out_grad, slot_tokens, slot_gate, w_gate, w_up, w_down):
    gate_weight, up_weight, down_weight = w_gate[0], w_up[0], w_down[0]
    send = call(
        dispatch_kernel,
        shape((OWNERS, 2 * ROOM, LANES), BF16),
        (slot_tokens, tokens, out_grad),
    )
    recv = lax.all_to_all(send, ("x", "y"), split_axis=0, concat_axis=0, tiled=True)
    halves = shape((BLOCKS, 3 * HALF, LANES), F32)
    rows = shape((CAP, LANES), BF16)
    keep, give, inputs, scaled = call(
        front_kernel,
        (halves, halves, rows, rows),
        (slot_tokens, slot_gate, recv, gate_weight, up_weight, down_weight),
    )
    sums = (keep + swap_cores(give)).astype(BF16)
    parts = lax.all_to_all(sums, "z", split_axis=0, concat_axis=0, tiled=True)
    piece = call(middle_kernel, shape((PIECE, LANES), BF16), (slot_gate, parts))
    mine = lax.all_gather(piece, "z", axis=0, tiled=False)
    other = swap_cores(mine)
    grad_gate, grad_up, grad_down, outgoing = call(
        back_kernel,
        (
            shape(gate_weight.shape, BF16),
            shape(up_weight.shape, BF16),
            shape(down_weight.shape, BF16),
            shape((OWNERS, ROOM, LANES), F32),
        ),
        (slot_tokens, inputs, scaled, mine, other, gate_weight, up_weight),
    )
    incoming = lax.all_to_all(outgoing, ("x", "y"), split_axis=0, concat_axis=0, tiled=True)
    grad_tokens, gate_line = call(
        last_kernel,
        (shape((TOK, LANES), BF16), shape((1, LANES), F32)),
        (slot_tokens, incoming),
    )
    return (grad_tokens, grad_gate[None], grad_up[None], grad_down[None], gate_line[:, :40])


def solution(mesh):
    torus = Mesh(mesh.devices.reshape(16, 2, 4, 4), ("z", "core", "x", "y"))
    dp, expert = ("z", "core"), ("x", "y")
    in_specs = (
        P(expert, dp),
        P(expert, dp),
        P(),
        P(),
        P(expert, dp, None),
        P(expert, dp, None),
        P(expert, None, dp),
    )
    out_specs = (
        P(expert, dp),
        P(expert, dp, None),
        P(expert, dp, None),
        P(expert, None, dp),
        P(expert, None),
    )
    return jax.shard_map(
        per_device, mesh=torus, in_specs=in_specs, out_specs=out_specs, check_vma=False
    )
```

time: 413 us -> 159 us (0.38)
  waiting for transfers between devices: 237 us -> 6.01 us
  blocking collectives: 45.9 us -> 114 us
  local copies, waits for them, and re-layouts: 68.4 us -> 1.01 us
  Pallas kernels: 0 us -> 15.8 us
  between operations: 14.4 us -> 0.65 us
  matrix products: 8.99 us -> 0 us
  other arithmetic: 9.11 us -> 1.91 us
  starting transfers between devices: 25.2 us -> 19.1 us
    psum x1 -> x0, waiting for transfers between devices: 225 us -> none  [per_device(): pre_gate, pre_up = lax.psum((part_gate, part_up), 'dp')]
    all_to_all x0 -> x3, blocking collectives: none -> 81.4 us  [the longest x1 55.7 us: per_device(): parts = lax.all_to_all(sums, 'z', split_axis=0, concat_axis=0, tiled=True)]
    scatter x3 -> x0, local copies, waits for them, and re-layouts: 60.7 us -> none  [the longest x1 29.9 us: per_device(): send_table = jnp.zeros((flight_count, bucket_size + 1), jnp.int32).at[exp...]
    psum x1 -> x0, blocking collectives: 45.9 us -> none  [per_device(): gate_total = lax.psum(gate_part, 'dp')]
    all_gather x0 -> x1, blocking collectives: none -> 32.2 us  [per_device(): mine = lax.all_gather(piece, 'z', axis=0, tiled=False)]
    all_to_all x3 -> x0, starting transfers between devices: 17.3 us -> none  [the longest x1 7.57 us: per_device(): lax.all_to_all(grad_send, 'expert', split_axis=0, concat_axis=0, tiled=True)]
    pallas_call x0 -> x5, Pallas kernels: none -> 15.8 us  [call(): pl.pallas_call(kernel, out_shape=out_shape, in_specs=[VMEM] * len(inputs)...]
    all_to_all x3 -> x0, waiting for transfers between devices: 11.9 us -> none  [the longest x1 6.55 us: per_device(): lax.all_to_all(grad_send, 'expert', split_axis=0, concat_axis=0, tiled=True)]
  transfers between devices with their start and end apart: 6 -> 2, of which waited for: 4 -> 2; matrix products, arithmetic and copies ran while one was open for 2% -> 0% of each run, Pallas kernels for 0% -> 0%
where the time goes in v1:
time: 159 us; the launch traced here: 158 us
  blocking collectives  114 us (72%)
  starting transfers between devices  19.1 us (12%)
  Pallas kernels  15.8 us (10%)
  waiting for transfers between devices  6.01 us (4%)
  other arithmetic  1.91 us (1%)
    all_to_all x1, blocking collectives, per_device(): parts = lax.all_to_all(sums, 'z', split_axis=0, concat_axis=0, tiled=True)  55.7 us
    all_gather x1, blocking collectives, per_device(): mine = lax.all_gather(piece, 'z', axis=0, tiled=False)  32.2 us
    ppermute x2, starting transfers between devices, swap_cores(): return lax.ppermute(value, 'core', [(0, 1), (1, 0)])  19.1 us
    pallas_call x5, Pallas kernels, call(): pl.pallas_call(kernel, out_shape=out_shape, in_specs=[VMEM] * len(inputs)...  15.8 us
    all_to_all x1, blocking collectives, per_device(): lax.all_to_all(send, ('x', 'y'), split_axis=0, concat_axis=0, tiled=True)  14.6 us
    all_to_all x1, blocking collectives, per_device(): lax.all_to_all(outgoing, ('x', 'y'), split_axis=0, concat_axis=0, tiled=T...  11.1 us
    ppermute x2, waiting for transfers between devices, swap_cores(): return lax.ppermute(value, 'core', [(0, 1), (1, 0)])  6.01 us
  transfers between devices with their start and end apart: 2, of which 2 were waited for; matrix products, arithmetic and copies ran while one was open for 0% of the time, Pallas kernels for 0%

profile of v1, /device:TPU:1, one launch (start us, length us, event | category | flops | bytes accessed | tf_op | source)
XLA Modules:
  0.0 158.1 jit_solution(4800666126303802387)
XLA Ops:
  0.6 2.1 %shard_map.110 = bf16[16,48,128]{2,1,0:T(8,128)(2,1)} custom-call(s32[4,160]{1,0:T(4,128)} %slots_ref.7, bf16[320,128]{1,0:T(8,128)(2,1)} %tokens_ref.1, bf16[320,128]{1,0:T(8,128)(2,1)} %grads_ref.1), custom_call_target="tpu_custom_call" | custom-call | tf_op jit(solution)/shard_map/pallas_call | solution.py:221
  2.7 14.6 %all_to_all.15.recv_ref = bf16[16,48,128]{2,1,0:T(8,128)(2,1)} all-to-all(bf16[16,48,128]{2,1,0:T(8,128)(2,1)} %shard_map.110), channel_id=1, replica_groups=mesh['z'=16,'core'=2,'x'=4,'y'=4] {'x','y'}, dimensions={0} | all-to-all | bytes 393216 | tf_op jit(solution)/shard_map/all_to_all | solution.py:244
  17.3 4.5 %shard_map.111 = (f32[16,240,128]{2,1,0:T(8,128)}, f32[16,240,128]{2,1,0:T(8,128)}, bf16[160,128]{1,0:T(8,128)(2,1)}, bf16[160,128]{1,0:T(8,128)(2,1)}) custom-call(s32[4,160]{1,0:T(4,128)} %slots_ref.7, f32[4,160]{1,0:T(4,128)} %gates_ref.3, bf16[16,48,128]{2,1,0:T(8,128)(2,1)} %all_to_all.15.recv_ref, bf16[128,2048]{1,0:T(8,128)(2,1)} %bitcast.10, ...), custom_call_target="tpu_custom_call" | custom-call | tf_op jit(solution)/shard_map/pallas_call | solution.py:221
  21.8 6.4 %collective-permute-start = (f32[16,240,128]{2,1,0:T(8,128)}, f32[16,240,128]{2,1,0:T(8,128)S(1)}, u32[]{:S(2)}, u32[]{:S(2)}) collective-permute-start(f32[16,240,128]{2,1,0:T(8,128)} %get-tuple-element.18), channel_id=1, source_target_pairs={{0,16},{16,0},{1,17},{17,1},{2,18},{18,2},{3,19},{19,3},{4,20},{20... | collective-permute-start | bytes 5898248 | tf_op jit(solution)/shard_map/ppermute | solution.py:234
  28.2 3.8 %collective-permute-done = f32[16,240,128]{2,1,0:T(8,128)S(1)} collective-permute-done((f32[16,240,128]{2,1,0:T(8,128)}, f32[16,240,128]{2,1,0:T(8,128)S(1)}, u32[]{:S(2)}, u32[]{:S(2)}) %collective-permute-start) | collective-permute-done | bytes 1966112 | tf_op jit(solution)/shard_map/ppermute | solution.py:234
  32.0 1.9 %add_convert_fusion = bf16[16,240,128]{2,1,0:T(8,128)(2,1)S(1)} fusion(f32[16,240,128]{2,1,0:T(8,128)} %get-tuple-element.17, f32[16,240,128]{2,1,0:T(8,128)S(1)} %collective-permute-done), kind=kLoop, calls=%fused_computation | loop fusion | flops 983040 | bytes 4915200 | tf_op jit(solution)/shard_map/convert_element_type | solution.py:252
  33.9 55.7 %all_to_all.16.parts_ref = bf16[16,240,128]{2,1,0:T(8,128)(2,1)} all-to-all(bf16[16,240,128]{2,1,0:T(8,128)(2,1)S(1)} %add_convert_fusion), channel_id=1, replica_groups=mesh['z'=16,'core'=2,'x'=4,'y'=4] {'z'}, dimensions={0} | all-to-all | bytes 1966080 | tf_op jit(solution)/shard_map/all_to_all | solution.py:253
  89.6 2.1 %shard_map.112 = bf16[248,128]{1,0:T(8,128)(2,1)} custom-call(f32[4,160]{1,0:T(4,128)} %gates_ref.3, bf16[16,240,128]{2,1,0:T(8,128)(2,1)} %all_to_all.16.parts_ref), custom_call_target="tpu_custom_call" | custom-call | tf_op jit(solution)/shard_map/pallas_call | solution.py:221
  91.7 32.2 %all-gather = bf16[3968,128]{1,0:T(8,128)(2,1)S(1)} all-gather(bf16[248,128]{1,0:T(8,128)(2,1)} %shard_map.112), channel_id=2, replica_groups=mesh['z'=16,'core'=2,'x'=4,'y'=4] {'z'}, dimensions={0}, use_global_device_ids=true | all-gather | bytes 1079296 | tf_op jit(solution)/shard_map/all_gather | solution.py:255
  123.9 0.0 copy-start
  123.9 12.7 %collective-permute-start.1 = (bf16[16,248,128]{2,1,0:T(8,128)(2,1)S(1)}, bf16[16,248,128]{2,1,0:T(8,128)(2,1)S(1)}, u32[]{:S(2)}, u32[]{:S(2)}) collective-permute-start(bf16[16,248,128]{2,1,0:T(8,128)(2,1)S(1)} %bitcast.8), channel_id=1, source_target_pairs={{0,16},{16,0},{1,17},{17,1},{2,18},{18,2},{3,19},{19,3},{4,20},{20... | collective-permute-start | bytes 3047432 | tf_op jit(solution)/shard_map/ppermute | solution.py:234
  136.6 2.2 %collective-permute-done.1.other_ref = bf16[16,248,128]{2,1,0:T(8,128)(2,1)S(1)} collective-permute-done((bf16[16,248,128]{2,1,0:T(8,128)(2,1)S(1)}, bf16[16,248,128]{2,1,0:T(8,128)(2,1)S(1)}, u32[]{:S(2)}, u32[]{:S(2)}) %collective-permute-start.1) | collective-permute-done | bytes 1015840 | tf_op jit(solution)/shard_map/ppermute | solution.py:234
  138.8 0.0 copy-start.1
  138.8 0.0 copy-done
  138.8 1.0 copy-done.1
  139.8 4.7 %shard_map.113 = (bf16[128,2048]{1,0:T(8,128)(2,1)}, bf16[128,2048]{1,0:T(8,128)(2,1)}, bf16[2048,128]{1,0:T(8,128)(2,1)}, f32[16,24,128]{2,1,0:T(8,128)}) custom-call(s32[4,160]{1,0:T(4,128)} %slots_ref.7, bf16[160,128]{1,0:T(8,128)(2,1)} %get-tuple-element.15.inputs_ref, bf16[160,128]{1,0:T(8,128)(2,1)} %get-tuple-element.16.scaled_ref, ...), custom_call_target="tpu_custom_call" | custom-call | tf_op jit(solution)/shard_map/pallas_call | solution.py:221
  144.5 11.1 %all_to_all.17.incoming_ref = f32[16,24,128]{2,1,0:T(8,128)} all-to-all(f32[16,24,128]{2,1,0:T(8,128)} %get-tuple-element.19), channel_id=1, replica_groups=mesh['z'=16,'core'=2,'x'=4,'y'=4] {'x','y'}, dimensions={0} | all-to-all | bytes 393216 | tf_op jit(solution)/shard_map/all_to_all | solution.py:267
  155.6 2.5 %shard_map.114 = (bf16[320,128]{1,0:T(8,128)(2,1)}, f32[1,128]{1,0:T(1,128)}) custom-call(s32[4,160]{1,0:T(4,128)} %slots_ref.7, f32[16,24,128]{2,1,0:T(8,128)} %all_to_all.17.incoming_ref), custom_call_target="tpu_custom_call" | custom-call | tf_op jit(solution)/shard_map/pallas_call | solution.py:221
Async XLA Ops:
  21.8 10.2 %collective-permute-start = (f32[16,240,128]{2,1,0:T(8,128)}, f32[16,240,128]{2,1,0:T(8,128)S(1)}, u32[]{:S(2)}, u32[]{:S(2)}) collective-permute-start(f32[16,240,128]{2,1,0:T(8,128)} %get-tuple-element.18), channel_id=1, source_target_pairs={{0,16},{16,0},{1,17},{17,1},{2,18},{18,2},{3,19},{19,3},{4,20},{20... | collective-permute-start | bytes 5898248 | tf_op jit(solution)/shard_map/ppermute | solution.py:234
  123.9 14.9 %copy-start = (bf16[3968,128]{1,0:T(8,128)(2,1)}, bf16[3968,128]{1,0:T(8,128)(2,1)S(1)}, u32[]{:S(2)}) copy-start(bf16[3968,128]{1,0:T(8,128)(2,1)S(1)} %all-gather) | copy-start | bytes 3047428
  123.9 14.9 %collective-permute-start.1 = (bf16[16,248,128]{2,1,0:T(8,128)(2,1)S(1)}, bf16[16,248,128]{2,1,0:T(8,128)(2,1)S(1)}, u32[]{:S(2)}, u32[]{:S(2)}) collective-permute-start(bf16[16,248,128]{2,1,0:T(8,128)(2,1)S(1)} %bitcast.8), channel_id=1, source_target_pairs={{0,16},{16,0},{1,17},{17,1},{2,18},{18,2},{3,19},{19,3},{4,20},{20... | collective-permute-start | bytes 3047432 | tf_op jit(solution)/shard_map/ppermute | solution.py:234
  138.8 1.0 copy-start.1

commit v2 on v1

--- a/solution.py
+++ b/solution.py
@@ -1,6 +1,5 @@
 import jax
 import jax.numpy as jnp
-import numpy as np
 from jax import lax
 from jax.experimental import pallas as pl
 from jax.experimental.pallas import tpu as pltpu
@@ -16,6 +15,7 @@
 HALF = 80
 OWNERS = 16
 FLIGHT = 4
+MOST = 20
 ROOM = 24
 LANES = 128
 BLOCKS = 16
@@ -38,10 +38,10 @@
     )
 
 
-def owned_tokens(row, first, rows):
+def owned_tokens(row, first, rows, room):
     start = jnp.sum((row < first).astype(I32), axis=1, keepdims=True)
     count = jnp.sum(((row >= first) & (row < first + TOK)).astype(I32), axis=1, keepdims=True)
-    rank = lax.rem(iota((rows, CAP), 0), ROOM)
+    rank = lax.rem(iota((rows, CAP), 0), room)
     chosen = (iota((rows, CAP), 1) == start + rank) & (rank < count)
     token = jnp.sum(jnp.where(chosen, row - first + 1, 0), axis=1, keepdims=True)
     return token - 1
@@ -66,11 +66,11 @@
 
 def dispatch_kernel(slots_ref, tokens_ref, grads_ref, send_ref):
     first = TOK * (4 * lax.axis_index("x") + lax.axis_index("y"))
-    rows = 2 * ROOM
+    rows = 2 * MOST
     for expert in range(FLIGHT):
-        local = owned_tokens(slots_ref[expert : expert + 1, :], first, rows)
+        local = owned_tokens(slots_ref[expert : expert + 1, :], first, rows, MOST)
         hit = local == iota((rows, TOK), 1)
-        upper = iota((rows, TOK), 0) < ROOM
+        upper = iota((rows, TOK), 0) < MOST
         pick_tokens = jnp.where(hit & upper, 1.0, 0.0).astype(BF16)
         pick_grads = jnp.where(hit & ~upper, 1.0, 0.0).astype(BF16)
         rows_out = (dot(pick_tokens, tokens_ref[...]) + dot(pick_grads, grads_ref[...])).astype(BF16)
@@ -85,12 +85,12 @@
     core = lax.axis_index("core")
     row = slots_ref[pl.ds(expert, 1), :]
     owner, rank = places(row, core)
-    place = owner * (2 * ROOM) + rank
-    width = OWNERS * 2 * ROOM
+    place = owner * (2 * MOST) + rank
+    width = OWNERS * 2 * MOST
     recv = recv_ref[...].reshape(width, LANES)
     where = iota((CAP, width), 1)
     inputs = dot(jnp.where(where == place, 1.0, 0.0).astype(BF16), recv).astype(BF16)
-    grads = dot(jnp.where(where == place + ROOM, 1.0, 0.0).astype(BF16), recv)
+    grads = dot(jnp.where(where == place + MOST, 1.0, 0.0).astype(BF16), recv)
     gates = column(gates_ref[pl.ds(expert, 1), :], core)
     scaled = (gates * grads).astype(BF16)
     inputs_ref[...] = inputs
@@ -110,16 +110,35 @@
                 send_ref[2 * pair + side, rows, :] = total[HALF:, lanes]
 
 
-def middle_kernel(gates_ref, parts_ref, out_ref):
+def pair_kernel(keep_ref, recv_ref, sums_ref, own_ref):
+    for block in range(BLOCKS):
+        sums_ref[block] = (keep_ref[block] + recv_ref[block]).astype(BF16)
+    first = 4 * lax.axis_index("zl")
+    for block in range(4):
+        own_ref[block] = keep_ref[first + block] + recv_ref[first + block]
+
+
+def others(parts_ref, axis, own, index):
+    here = lax.axis_index(axis)
+    for step in range(1, 4):
+        own = own + parts_ref[(lax.rem(here + step, 4), *index)].astype(F32)
+    return own
+
+
+def near_kernel(parts_ref, own_ref, sums_ref, left_ref):
+    for block in range(4):
+        sums_ref[block] = others(parts_ref, "zl", own_ref[block], (block,)).astype(BF16)
+    block = lax.axis_index("zh")
+    left_ref[...] = others(parts_ref, "zl", own_ref[block], (block,))
+
+
+def middle_kernel(gates_ref, parts_ref, own_ref, out_ref):
     core = lax.axis_index("core")
     gates = column(gates_ref[pl.ds(lax.axis_index("x"), 1), :], core)[:HALF]
 
     def total(which):
         rows = slice(HALF * which, HALF * which + HALF)
-        result = parts_ref[0, rows, :].astype(F32)
-        for block in range(1, BLOCKS):
-            result = result + parts_ref[block, rows, :].astype(F32)
-        return result
+        return others(parts_ref, "zh", own_ref[rows, :], (rows,))
 
     pre_gate, pre_up, upstream = total(0), total(1), total(2)
     sigmoid = jax.nn.sigmoid(pre_gate)
@@ -134,6 +153,10 @@
     line = iota((8, LANES), 0)
     tail = jnp.where(line == 0, high, jnp.where(line == 1, part - high, 0.0))
     out_ref[3 * HALF :, :] = tail.astype(BF16)
+
+
+def holder(block):
+    return 4 * (block % 4) + block // 4
 
 
 def back_kernel(
@@ -156,8 +179,8 @@
     def joined(which, pair):
         rows = slice(HALF * which, HALF * which + HALF)
         sides = [
-            jnp.concatenate([mine_ref[block, rows, :], other_ref[block, rows, :]], axis=0)
-            for block in (2 * pair, 2 * pair + 1)
+            jnp.concatenate([mine_ref[place, rows, :], other_ref[place, rows, :]], axis=0)
+            for place in (holder(2 * pair), holder(2 * pair + 1))
         ]
         return jnp.concatenate(sides, axis=1)
 
@@ -204,7 +227,7 @@
     first = TOK * (4 * expert_here + lax.axis_index("y"))
     total = jnp.zeros((TOK, LANES), F32)
     for expert in range(FLIGHT):
-        local = owned_tokens(slots_ref[expert : expert + 1, :], first, ROOM)
+        local = owned_tokens(slots_ref[expert : expert + 1, :], first, ROOM, ROOM)
         pick = jnp.where(local == iota((ROOM, TOK), 1), 1.0, 0.0)
         rows = incoming_ref[4 * expert]
         for part in range(1, 4):
@@ -223,11 +246,20 @@
         out_shape=out_shape,
         in_specs=[VMEM] * len(inputs),
         out_specs=jax.tree.map(lambda _: VMEM, out_shape),
+        compiler_params=pltpu.CompilerParams(vmem_limit_bytes=24 << 20),
     )(*inputs)
 
 
 def shape(dims, kind):
     return jax.ShapeDtypeStruct(dims, kind)
+
+
+def on_chip(dims, kind):
+    return pltpu.VMEM(dims, kind)
+
+
+def near(value):
+    return pltpu.with_memory_space_constraint(value, pltpu.VMEM)
 
 
 def swap_cores(value):
@@ -238,21 +270,31 @@
     gate_weight, up_weight, down_weight = w_gate[0], w_up[0], w_down[0]
     send = call(
         dispatch_kernel,
-        shape((OWNERS, 2 * ROOM, LANES), BF16),
+        on_chip((OWNERS, 2 * MOST, LANES), BF16),
         (slot_tokens, tokens, out_grad),
     )
     recv = lax.all_to_all(send, ("x", "y"), split_axis=0, concat_axis=0, tiled=True)
-    halves = shape((BLOCKS, 3 * HALF, LANES), F32)
-    rows = shape((CAP, LANES), BF16)
+    halves = on_chip((BLOCKS, 3 * HALF, LANES), F32)
+    rows = on_chip((CAP, LANES), BF16)
     keep, give, inputs, scaled = call(
         front_kernel,
         (halves, halves, rows, rows),
-        (slot_tokens, slot_gate, recv, gate_weight, up_weight, down_weight),
-    )
-    sums = (keep + swap_cores(give)).astype(BF16)
-    parts = lax.all_to_all(sums, "z", split_axis=0, concat_axis=0, tiled=True)
-    piece = call(middle_kernel, shape((PIECE, LANES), BF16), (slot_gate, parts))
-    mine = lax.all_gather(piece, "z", axis=0, tiled=False)
+        (slot_tokens, slot_gate, near(recv), gate_weight, up_weight, down_weight),
+    )
+    sums, own = call(
+        pair_kernel,
+        (on_chip((BLOCKS, 3 * HALF, LANES), BF16), on_chip((4, 3 * HALF, LANES), F32)),
+        (near(keep), near(swap_cores(give))),
+    )
+    parts = lax.all_to_all(sums.reshape(4, 4, 3 * HALF, LANES), "zl", split_axis=0, concat_axis=0, tiled=True)
+    sums, own = call(
+        near_kernel,
+        (on_chip((4, 3 * HALF, LANES), BF16), on_chip((3 * HALF, LANES), F32)),
+        (near(parts), near(own)),
+    )
+    parts = lax.all_to_all(sums, "zh", split_axis=0, concat_axis=0, tiled=True)
+    piece = call(middle_kernel, on_chip((PIECE, LANES), BF16), (slot_gate, near(parts), near(own)))
+    mine = lax.all_gather(piece, ("zh", "zl"), axis=0, tiled=False)
     other = swap_cores(mine)
     grad_gate, grad_up, grad_down, outgoing = call(
         back_kernel,
@@ -260,22 +302,22 @@
             shape(gate_weight.shape, BF16),
             shape(up_weight.shape, BF16),
             shape(down_weight.shape, BF16),
-            shape((OWNERS, ROOM, LANES), F32),
+            on_chip((OWNERS, ROOM, LANES), F32),
         ),
-        (slot_tokens, inputs, scaled, mine, other, gate_weight, up_weight),
+        (slot_tokens, near(inputs), near(scaled), near(mine), near(other), gate_weight, up_weight),
     )
     incoming = lax.all_to_all(outgoing, ("x", "y"), split_axis=0, concat_axis=0, tiled=True)
     grad_tokens, gate_line = call(
         last_kernel,
         (shape((TOK, LANES), BF16), shape((1, LANES), F32)),
-        (slot_tokens, incoming),
+        (slot_tokens, near(incoming)),
     )
     return (grad_tokens, grad_gate[None], grad_up[None], grad_down[None], gate_line[:, :40])
 
 
 def solution(mesh):
-    torus = Mesh(mesh.devices.reshape(16, 2, 4, 4), ("z", "core", "x", "y"))
-    dp, expert = ("z", "core"), ("x", "y")
+    torus = Mesh(mesh.devices.reshape(4, 4, 2, 4, 4), ("zh", "zl", "core", "x", "y"))
+    dp, expert = ("zh", "zl", "core"), ("x", "y")
     in_specs = (
         P(expert, dp),
         P(expert, dp),

time: 159 us -> 145 us (0.912)
  Pallas kernels: 15.8 us -> 6.07 us
  local copies, waits for them, and re-layouts: 1.01 us -> 6.28 us
  blocking collectives: 114 us -> 109 us
  starting transfers between devices: 19.1 us -> 17 us
  other arithmetic: 1.91 us -> 0 us
    pallas_call x5 -> x7, Pallas kernels: 15.8 us -> 6.07 us  [call(): pl.pallas_call(kernel, out_shape=out_shape, in_specs=[VMEM] * len(inputs)...]
    unnamed x4 -> x22, local copies, waits for them, and re-layouts: 1.01 us -> 6.28 us
    all_gather x1, blocking collectives: 32.2 us -> 29.4 us  [per_device(): mine = lax.all_gather(piece, ('zh', 'zl'), axis=0, tiled=False)]
    ppermute x2, starting transfers between devices: 19.1 us -> 17 us  [swap_cores(): return lax.ppermute(value, 'core', [(0, 1), (1, 0)])]
    convert_element_type x1 -> x0, other arithmetic: 1.91 us -> none  [per_device(): sums = (keep + swap_cores(give)).astype(BF16)]
    all_to_all x1 -> x2, blocking collectives: 55.7 us -> 55 us  [the longest x1 28.1 us: per_device(): lax.all_to_all(sums.reshape(4, 4, 3 * HALF, LANES), 'zl', split_axis=0, c...]
where the time goes in v2:
time: 145 us
  blocking collectives  109 us (75%)
  starting transfers between devices  17 us (12%)
  local copies, waits for them, and re-layouts  6.28 us (4%)
  Pallas kernels  6.07 us (4%)
  waiting for transfers between devices  5.79 us (4%)
    all_gather x1, blocking collectives, per_device(): mine = lax.all_gather(piece, ('zh', 'zl'), axis=0, tiled=False)  29.4 us
    all_to_all x1, blocking collectives, per_device(): lax.all_to_all(sums.reshape(4, 4, 3 * HALF, LANES), 'zl', split_axis=0, c...  28.1 us
    all_to_all x1, blocking collectives, per_device(): parts = lax.all_to_all(sums, 'zh', split_axis=0, concat_axis=0, tiled=True)  26.9 us
    ppermute x2, starting transfers between devices, swap_cores(): return lax.ppermute(value, 'core', [(0, 1), (1, 0)])  17 us
    all_to_all x1, blocking collectives, per_device(): lax.all_to_all(send, ('x', 'y'), split_axis=0, concat_axis=0, tiled=True)  14.3 us
    all_to_all x1, blocking collectives, per_device(): lax.all_to_all(outgoing, ('x', 'y'), split_axis=0, concat_axis=0, tiled=T...  10.2 us
    unnamed x22, local copies, waits for them, and re-layouts  6.28 us
    pallas_call x7, Pallas kernels, call(): pl.pallas_call(kernel, out_shape=out_shape, in_specs=[VMEM] * len(inputs)...  6.07 us
  transfers between devices with their start and end apart: 2, of which 2 were waited for; matrix products, arithmetic and copies ran while one was open for 0% of the time, Pallas kernels for 0%

profile of v2, /device:TPU:1, one launch (start us, length us, event | category | flops | bytes accessed | tf_op | source)
XLA Modules:
  0.0 144.7 jit_solution(4581148015184461197)
XLA Ops:
  0.6 0.0 copy-start.5
  0.6 0.9 copy-done.5
  1.5 0.0 copy-start.6
  1.5 0.9 copy-done.6
  2.4 0.0 copy-start.7
  2.4 0.7 copy-done.7
  3.1 0.5 shard_map.110
  3.6 14.3 %all_to_all.20.recv_ref = bf16[16,40,128]{2,1,0:T(8,128)(2,1)S(1)} all-to-all(bf16[16,40,128]{2,1,0:T(8,128)(2,1)S(1)} %shard_map.110), channel_id=1, replica_groups=mesh['zh'=4,'zl'=4,'core'=2,'x'=4,'y'=4] {'x','y'}, dimensions={0} | all-to-all | bytes 327680 | tf_op jit(solution)/shard_map/all_to_all | solution.py:276
  17.9 0.0 copy-start
  17.9 1.0 copy-done
  18.9 1.0 copy-done.2
  19.9 1.0 copy-done.4
  21.0 0.7 copy-done.9
  21.7 1.1 shard_map.111
  22.8 5.0 %collective-permute-start = (f32[16,240,128]{2,1,0:T(8,128)S(1)}, f32[16,240,128]{2,1,0:T(8,128)S(1)}, u32[]{:S(2)}, u32[]{:S(2)}) collective-permute-start(f32[16,240,128]{2,1,0:T(8,128)S(1)} %get-tuple-element.22), channel_id=1, source_target_pairs={{0,16},{16,0},{1,17},{17,1},{2,18},{18,2},{3,19},{19,3},{4,20},{20... | collective-permute-start | bytes 5898248 | tf_op jit(solution)/shard_map/ppermute | solution.py:266
  27.8 3.6 %collective-permute-done.recv_ref = f32[16,240,128]{2,1,0:T(8,128)S(1)} collective-permute-done((f32[16,240,128]{2,1,0:T(8,128)S(1)}, f32[16,240,128]{2,1,0:T(8,128)S(1)}, u32[]{:S(2)}, u32[]{:S(2)}) %collective-permute-start) | collective-permute-done | bytes 1966112 | tf_op jit(solution)/shard_map/ppermute | solution.py:266
  31.4 0.4 shard_map.112
  31.8 0.0 copy-start.10
  31.8 28.1 %all_to_all.21.parts_ref = bf16[4,4,240,128]{3,2,1,0:T(8,128)(2,1)S(1)} all-to-all(bf16[4,4,240,128]{3,2,1,0:T(8,128)(2,1)S(1)} %bitcast.15), channel_id=1, replica_groups=mesh['zh'=4,'zl'=4,'core'=2,'x'=4,'y'=4] {'zl'}, dimensions={0} | all-to-all | bytes 1966080 | tf_op jit(solution)/shard_map/all_to_all | solution.py:289
  59.9 0.1 shard_map.113
  60.1 26.9 %all_to_all.22.parts_ref = bf16[4,240,128]{2,1,0:T(8,128)(2,1)S(1)} all-to-all(bf16[4,240,128]{2,1,0:T(8,128)(2,1)S(1)} %get-tuple-element.25), channel_id=1, replica_groups=mesh['zh'=4,'zl'=4,'core'=2,'x'=4,'y'=4] {'zh'}, dimensions={0} | all-to-all | bytes 491520 | tf_op jit(solution)/shard_map/all_to_all | solution.py:295
  87.0 0.0 copy-done.10
  87.0 0.2 shard_map.114
  87.2 29.4 %all-gather = bf16[3968,128]{1,0:T(8,128)(2,1)S(1)} all-gather(bf16[248,128]{1,0:T(8,128)(2,1)S(1)} %shard_map.114), channel_id=2, replica_groups=mesh['zh'=4,'zl'=4,'core'=2,'x'=4,'y'=4] {'zh','zl'}, dimensions={0}, use_global_device_ids=true | all-gather | bytes 1079296 | tf_op jit(solution)/shard_map/all_gather | solution.py:297
  116.6 12.0 %collective-permute-start.1 = (bf16[16,248,128]{2,1,0:T(8,128)(2,1)S(1)}, bf16[16,248,128]{2,1,0:T(8,128)(2,1)S(1)}, u32[]{:S(2)}, u32[]{:S(2)}) collective-permute-start(bf16[16,248,128]{2,1,0:T(8,128)(2,1)S(1)} %bitcast.9), channel_id=1, source_target_pairs={{0,16},{16,0},{1,17},{17,1},{2,18},{18,2},{3,19},{19,3},{4,20},{20... | collective-permute-start | bytes 3047432 | tf_op jit(solution)/shard_map/ppermute | solution.py:266
  128.5 2.2 %collective-permute-done.1.other_ref = bf16[16,248,128]{2,1,0:T(8,128)(2,1)S(1)} collective-permute-done((bf16[16,248,128]{2,1,0:T(8,128)(2,1)S(1)}, bf16[16,248,128]{2,1,0:T(8,128)(2,1)S(1)}, u32[]{:S(2)}, u32[]{:S(2)}) %collective-permute-start.1) | collective-permute-done | bytes 1015840 | tf_op jit(solution)/shard_map/ppermute | solution.py:266
  130.8 0.0 copy-done.1
  130.8 0.0 copy-done.3
  130.8 0.0 copy-done.8
  130.8 2.2 %shard_map.115 = (bf16[128,2048]{1,0:T(8,128)(2,1)}, bf16[128,2048]{1,0:T(8,128)(2,1)}, bf16[2048,128]{1,0:T(8,128)(2,1)}, f32[16,24,128]{2,1,0:T(8,128)S(1)}) custom-call(s32[4,160]{1,0:T(4,128)S(1)} %copy-done.8, bf16[160,128]{1,0:T(8,128)(2,1)S(1)} %get-tuple-element.19.inputs_ref, bf16[160,128]{1,0:T(8,128)(2,1)S(1)} %get-tuple-element.20.scaled_ref, ...), custom_call_target="tpu_custom_call" | custom-call | tf_op jit(solution)/shard_map/pallas_call | solution.py:244
  133.0 10.2 %all_to_all.23.incoming_ref = f32[16,24,128]{2,1,0:T(8,128)S(1)} all-to-all(f32[16,24,128]{2,1,0:T(8,128)S(1)} %get-tuple-element.27), channel_id=1, replica_groups=mesh['zh'=4,'zl'=4,'core'=2,'x'=4,'y'=4] {'x','y'}, dimensions={0} | all-to-all | bytes 393216 | tf_op jit(solution)/shard_map/all_to_all | solution.py:309
  143.2 1.6 %shard_map.116 = (bf16[320,128]{1,0:T(8,128)(2,1)}, f32[1,128]{1,0:T(1,128)}) custom-call(s32[4,160]{1,0:T(4,128)S(1)} %copy-done.8, f32[16,24,128]{2,1,0:T(8,128)S(1)} %all_to_all.23.incoming_ref), custom_call_target="tpu_custom_call" | custom-call | tf_op jit(solution)/shard_map/pallas_call | solution.py:244
  (6 shorter events, 0.0 us)
Async XLA Ops:
  0.6 0.9 copy-start.5
  1.5 0.9 copy-start.6
  2.4 0.7 copy-start.7
  17.9 1.0 copy-start
  18.9 1.0 copy-start.2
  19.9 1.0 copy-start.4
  21.0 0.7 copy-start.9
  22.8 8.6 %collective-permute-start = (f32[16,240,128]{2,1,0:T(8,128)S(1)}, f32[16,240,128]{2,1,0:T(8,128)S(1)}, u32[]{:S(2)}, u32[]{:S(2)}) collective-permute-start(f32[16,240,128]{2,1,0:T(8,128)S(1)} %get-tuple-element.22), channel_id=1, source_target_pairs={{0,16},{16,0},{1,17},{17,1},{2,18},{18,2},{3,19},{19,3},{4,20},{20... | collective-permute-start | bytes 5898248 | tf_op jit(solution)/shard_map/ppermute | solution.py:266
  31.8 55.2 %copy-start.10 = (f32[4,160]{1,0:T(4,128)S(1)}, f32[4,160]{1,0:T(4,128)}, u32[]{:S(2)}) copy-start(f32[4,160]{1,0:T(4,128)} %gates_ref.3) | copy-start | bytes 7684
  59.9 70.8 %copy-start.1 = (bf16[1,128,2048]{2,1,0:T(8,128)(2,1)S(1)}, bf16[1,128,2048]{2,1,0:T(8,128)(2,1)}, u32[]{:S(2)}) copy-start(bf16[1,128,2048]{2,1,0:T(8,128)(2,1)} %param.11) | copy-start | bytes 1572868
  59.9 70.8 %copy-start.3 = (bf16[1,128,2048]{2,1,0:T(8,128)(2,1)S(1)}, bf16[1,128,2048]{2,1,0:T(8,128)(2,1)}, u32[]{:S(2)}) copy-start(bf16[1,128,2048]{2,1,0:T(8,128)(2,1)} %param.12) | copy-start | bytes 1572868
  59.9 70.8 %copy-start.8 = (s32[4,160]{1,0:T(4,128)S(1)}, s32[4,160]{1,0:T(4,128)}, u32[]{:S(2)}) copy-start(s32[4,160]{1,0:T(4,128)} %slots_ref.7) | copy-start | bytes 7684
  116.6 14.2 %collective-permute-start.1 = (bf16[16,248,128]{2,1,0:T(8,128)(2,1)S(1)}, bf16[16,248,128]{2,1,0:T(8,128)(2,1)S(1)}, u32[]{:S(2)}, u32[]{:S(2)}) collective-permute-start(bf16[16,248,128]{2,1,0:T(8,128)(2,1)S(1)} %bitcast.9), channel_id=1, source_target_pairs={{0,16},{16,0},{1,17},{17,1},{2,18},{18,2},{3,19},{19,3},{4,20},{20... | collective-permute-start | bytes 3047432 | tf_op jit(solution)/shard_map/ppermute | solution.py:266

commit v3 on v2

--- a/solution.py
+++ b/solution.py
@@ -21,6 +21,7 @@
 BLOCKS = 16
 PIECE = 3 * HALF + 8
 
+Z = ("pair", "odd")
 VMEM = pl.BlockSpec(memory_space=pltpu.VMEM)
 
 
@@ -64,7 +65,38 @@
     return owner, slot - start
 
 
-def dispatch_kernel(slots_ref, tokens_ref, grads_ref, send_ref):
+def dispatch_kernel(
+    slots_hbm,
+    gates_hbm,
+    tokens_hbm,
+    grads_hbm,
+    gate_hbm,
+    up_hbm,
+    down_hbm,
+    send_ref,
+    slots_ref,
+    gates_ref,
+    gate_ref,
+    up_ref,
+    down_ref,
+    tokens_ref,
+    grads_ref,
+    sems,
+):
+    pairs = (
+        (slots_hbm, slots_ref),
+        (tokens_hbm, tokens_ref),
+        (grads_hbm, grads_ref),
+        (gates_hbm, gates_ref),
+        (gate_hbm, gate_ref),
+        (up_hbm, up_ref),
+        (down_hbm, down_ref),
+    )
+    copies = [pltpu.make_async_copy(source, target, sems.at[i]) for i, (source, target) in enumerate(pairs)]
+    for copy in copies:
+        copy.start()
+    for copy in copies[:3]:
+        copy.wait()
     first = TOK * (4 * lax.axis_index("x") + lax.axis_index("y"))
     rows = 2 * MOST
     for expert in range(FLIGHT):
@@ -76,6 +108,8 @@
         rows_out = (dot(pick_tokens, tokens_ref[...]) + dot(pick_grads, grads_ref[...])).astype(BF16)
         for part in range(4):
             send_ref[4 * expert + part] = rows_out
+    for copy in copies[3:]:
+        copy.wait()
 
 
 def front_kernel(
@@ -110,26 +144,33 @@
                 send_ref[2 * pair + side, rows, :] = total[HALF:, lanes]
 
 
-def pair_kernel(keep_ref, recv_ref, sums_ref, own_ref):
-    for block in range(BLOCKS):
-        sums_ref[block] = (keep_ref[block] + recv_ref[block]).astype(BF16)
-    first = 4 * lax.axis_index("zl")
-    for block in range(4):
-        own_ref[block] = keep_ref[first + block] + recv_ref[first + block]
-
-
-def others(parts_ref, axis, own, index):
-    here = lax.axis_index(axis)
-    for step in range(1, 4):
-        own = own + parts_ref[(lax.rem(here + step, 4), *index)].astype(F32)
-    return own
-
-
-def near_kernel(parts_ref, own_ref, sums_ref, left_ref):
-    for block in range(4):
-        sums_ref[block] = others(parts_ref, "zl", own_ref[block], (block,)).astype(BF16)
-    block = lax.axis_index("zh")
-    left_ref[...] = others(parts_ref, "zl", own_ref[block], (block,))
+def chip():
+    return 2 * lax.axis_index("pair") + lax.axis_index("odd")
+
+
+def pair_kernel(keep_ref, recv_ref, right_ref, left_ref, even_ref):
+    def both(distance):
+        block = lax.rem(chip() + distance + BLOCKS, BLOCKS)
+        return keep_ref[block] + recv_ref[block]
+
+    for step in range(4):
+        right_ref[step] = both(1 + 2 * step).astype(BF16)
+        left_ref[step] = both(-1 - 2 * step).astype(BF16)
+    for step in range(8):
+        even_ref[step] = both(2 * step)
+
+
+def near_kernel(even_ref, from_left_ref, from_right_ref, sums_ref, own_ref):
+    here = lax.axis_index("pair")
+    for step in range(8):
+        total = even_ref[step]
+        if step < 4:
+            total = total + from_left_ref[step].astype(F32)
+        if step == 0 or step > 4:
+            total = total + from_right_ref[(8 - step) % 8].astype(F32)
+        if step == 0:
+            own_ref[...] = total
+        sums_ref[lax.rem(here + step, 8)] = total.astype(BF16)
 
 
 def middle_kernel(gates_ref, parts_ref, own_ref, out_ref):
@@ -138,7 +179,10 @@
 
     def total(which):
         rows = slice(HALF * which, HALF * which + HALF)
-        return others(parts_ref, "zh", own_ref[rows, :], (rows,))
+        result = own_ref[rows, :]
+        for step in range(1, 8):
+            result = result + parts_ref[lax.rem(lax.axis_index("pair") + step, 8), rows, :].astype(F32)
+        return result
 
     pre_gate, pre_up, upstream = total(0), total(1), total(2)
     sigmoid = jax.nn.sigmoid(pre_gate)
@@ -153,10 +197,6 @@
     line = iota((8, LANES), 0)
     tail = jnp.where(line == 0, high, jnp.where(line == 1, part - high, 0.0))
     out_ref[3 * HALF :, :] = tail.astype(BF16)
-
-
-def holder(block):
-    return 4 * (block % 4) + block // 4
 
 
 def back_kernel(
@@ -180,7 +220,7 @@
         rows = slice(HALF * which, HALF * which + HALF)
         sides = [
             jnp.concatenate([mine_ref[place, rows, :], other_ref[place, rows, :]], axis=0)
-            for place in (holder(2 * pair), holder(2 * pair + 1))
+            for place in (2 * pair, 2 * pair + 1)
         ]
         return jnp.concatenate(sides, axis=1)
 
@@ -266,12 +306,36 @@
     return lax.ppermute(value, "core", [(0, 1), (1, 0)])
 
 
+def far(value):
+    return pltpu.with_memory_space_constraint(value, pltpu.HBM)
+
+
+def shift(value, step):
+    return lax.ppermute(value, Z, [(z, (z + step) % BLOCKS) for z in range(BLOCKS)])
+
+
 def per_device(tokens, out_grad, slot_tokens, slot_gate, w_gate, w_up, w_down):
-    gate_weight, up_weight, down_weight = w_gate[0], w_up[0], w_down[0]
-    send = call(
+    send, slots, gates, gate_weight, up_weight, down_weight = pl.pallas_call(
         dispatch_kernel,
-        on_chip((OWNERS, 2 * MOST, LANES), BF16),
-        (slot_tokens, tokens, out_grad),
+        out_shape=(
+            on_chip((OWNERS, 2 * MOST, LANES), BF16),
+            on_chip(slot_tokens.shape, I32),
+            on_chip(slot_gate.shape, F32),
+            on_chip(w_gate.shape[1:], BF16),
+            on_chip(w_up.shape[1:], BF16),
+            on_chip(w_down.shape[1:], BF16),
+        ),
+        in_specs=[pl.BlockSpec(memory_space=pltpu.HBM)] * 7,
+        out_specs=(VMEM,) * 6,
+        scratch_shapes=[
+            pltpu.VMEM(tokens.shape, BF16),
+            pltpu.VMEM(tokens.shape, BF16),
+            pltpu.SemaphoreType.DMA((7,)),
+        ],
+        compiler_params=pltpu.CompilerParams(vmem_limit_bytes=24 << 20),
+    )(*(far(value) for value in (slot_tokens, slot_gate, tokens, out_grad, w_gate[0], w_up[0], w_down[0])))
+    slots, gates, gate_weight, up_weight, down_weight = (
+        near(value) for value in (slots, gates, gate_weight, up_weight, down_weight)
     )
     recv = lax.all_to_all(send, ("x", "y"), split_axis=0, concat_axis=0, tiled=True)
     halves = on_chip((BLOCKS, 3 * HALF, LANES), F32)
@@ -279,22 +343,23 @@
     keep, give, inputs, scaled = call(
         front_kernel,
         (halves, halves, rows, rows),
-        (slot_tokens, slot_gate, near(recv), gate_weight, up_weight, down_weight),
-    )
-    sums, own = call(
+        (slots, gates, near(recv), gate_weight, up_weight, down_weight),
+    )
+    quarter = on_chip((4, 3 * HALF, LANES), BF16)
+    right, left, even = call(
         pair_kernel,
-        (on_chip((BLOCKS, 3 * HALF, LANES), BF16), on_chip((4, 3 * HALF, LANES), F32)),
+        (quarter, quarter, on_chip((8, 3 * HALF, LANES), F32)),
         (near(keep), near(swap_cores(give))),
     )
-    parts = lax.all_to_all(sums.reshape(4, 4, 3 * HALF, LANES), "zl", split_axis=0, concat_axis=0, tiled=True)
+    from_left, from_right = shift(right, 1), shift(left, -1)
     sums, own = call(
         near_kernel,
-        (on_chip((4, 3 * HALF, LANES), BF16), on_chip((3 * HALF, LANES), F32)),
-        (near(parts), near(own)),
-    )
-    parts = lax.all_to_all(sums, "zh", split_axis=0, concat_axis=0, tiled=True)
-    piece = call(middle_kernel, on_chip((PIECE, LANES), BF16), (slot_gate, near(parts), near(own)))
-    mine = lax.all_gather(piece, ("zh", "zl"), axis=0, tiled=False)
+        (on_chip((8, 3 * HALF, LANES), BF16), on_chip((3 * HALF, LANES), F32)),
+        (near(even), near(from_left), near(from_right)),
+    )
+    parts = lax.all_to_all(sums, "pair", split_axis=0, concat_axis=0, tiled=True)
+    piece = call(middle_kernel, on_chip((PIECE, LANES), BF16), (gates, near(parts), near(own)))
+    mine = lax.all_gather(piece, Z, axis=0, tiled=False)
     other = swap_cores(mine)
     grad_gate, grad_up, grad_down, outgoing = call(
         back_kernel,
@@ -304,20 +369,20 @@
             shape(down_weight.shape, BF16),
             on_chip((OWNERS, ROOM, LANES), F32),
         ),
-        (slot_tokens, near(inputs), near(scaled), near(mine), near(other), gate_weight, up_weight),
+        (slots, near(inputs), near(scaled), near(mine), near(other), gate_weight, up_weight),
     )
     incoming = lax.all_to_all(outgoing, ("x", "y"), split_axis=0, concat_axis=0, tiled=True)
     grad_tokens, gate_line = call(
         last_kernel,
         (shape((TOK, LANES), BF16), shape((1, LANES), F32)),
-        (slot_tokens, near(incoming)),
+        (slots, near(incoming)),
     )
     return (grad_tokens, grad_gate[None], grad_up[None], grad_down[None], gate_line[:, :40])
 
 
 def solution(mesh):
-    torus = Mesh(mesh.devices.reshape(4, 4, 2, 4, 4), ("zh", "zl", "core", "x", "y"))
-    dp, expert = ("zh", "zl", "core"), ("x", "y")
+    torus = Mesh(mesh.devices.reshape(8, 2, 2, 4, 4), ("pair", "odd", "core", "x", "y"))
+    dp, expert = (*Z, "core"), ("x", "y")
     in_specs = (
         P(expert, dp),
         P(expert, dp),

time: 145 us -> 135 us (0.931)
  blocking collectives: 109 us -> 88.6 us
  starting transfers between devices: 17 us -> 27.4 us
  local copies, waits for them, and re-layouts: 6.28 us -> 0 us
  waiting for transfers between devices: 5.79 us -> 10.7 us
    all_to_all x2 -> x1, blocking collectives: 55 us -> 30.2 us  [per_device(): lax.all_to_all(sums, 'pair', split_axis=0, concat_axis=0, tiled=True)]
    ppermute x0 -> x2, starting transfers between devices: none -> 12 us  [shift(): lax.ppermute(value, Z, [(z, (z + step) % BLOCKS) for z in range(BLOCKS)])]
    unnamed x22 -> x0, local copies, waits for them, and re-layouts: 6.28 us -> none
    ppermute x0 -> x2, waiting for transfers between devices: none -> 4.92 us  [shift(): lax.ppermute(value, Z, [(z, (z + step) % BLOCKS) for z in range(BLOCKS)])]
    all_gather x1, blocking collectives: 29.4 us -> 33.9 us  [per_device(): mine = lax.all_gather(piece, Z, axis=0, tiled=False)]
    ppermute x2, starting transfers between devices: 17 us -> 15.4 us  [swap_cores(): return lax.ppermute(value, 'core', [(0, 1), (1, 0)])]
    pallas_call x0 -> x1, Pallas kernels: none -> 1.54 us  [per_device(): pl.pallas_call(dispatch_kernel, out_shape=(on_chip((OWNERS, 2 * MOST, LAN...]
    pallas_call x7 -> x6, Pallas kernels: 6.07 us -> 5.47 us  [call(): pl.pallas_call(kernel, out_shape=out_shape, in_specs=[VMEM] * len(inputs)...]
  transfers between devices with their start and end apart: 2 -> 4, of which waited for: 2 -> 4; matrix products, arithmetic and copies ran while one was open for 0% -> 0% of each run, Pallas kernels for 0% -> 0%
where the time goes in v3:
time: 135 us; the launch traced here: 134 us
  blocking collectives  88.6 us (66%)
  starting transfers between devices  27.4 us (20%)
  waiting for transfers between devices  10.7 us (8%)
  Pallas kernels  7 us (5%)
    all_gather x1, blocking collectives, per_device(): mine = lax.all_gather(piece, Z, axis=0, tiled=False)  33.9 us
    all_to_all x1, blocking collectives, per_device(): lax.all_to_all(sums, 'pair', split_axis=0, concat_axis=0, tiled=True)  30.2 us
    ppermute x2, starting transfers between devices, swap_cores(): return lax.ppermute(value, 'core', [(0, 1), (1, 0)])  15.4 us
    all_to_all x1, blocking collectives, per_device(): lax.all_to_all(send, ('x', 'y'), split_axis=0, concat_axis=0, tiled=True)  14.3 us
    ppermute x2, starting transfers between devices, shift(): lax.ppermute(value, Z, [(z, (z + step) % BLOCKS) for z in range(BLOCKS)])  12 us
    all_to_all x1, blocking collectives, per_device(): lax.all_to_all(outgoing, ('x', 'y'), split_axis=0, concat_axis=0, tiled=T...  10.2 us
    ppermute x2, waiting for transfers between devices, swap_cores(): return lax.ppermute(value, 'core', [(0, 1), (1, 0)])  5.79 us
    pallas_call x6, Pallas kernels, call(): pl.pallas_call(kernel, out_shape=out_shape, in_specs=[VMEM] * len(inputs)...  5.47 us
  transfers between devices with their start and end apart: 4, of which 4 were waited for; matrix products, arithmetic and copies ran while one was open for 0% of the time, Pallas kernels for 0%

profile of v3, /device:TPU:1, one launch (start us, length us, event | category | flops | bytes accessed | tf_op | source)
XLA Modules:
  0.0 134.4 jit_solution(16325730632266915160)
XLA Ops:
  0.6 1.5 %shard_map.110 = (bf16[16,40,128]{2,1,0:T(8,128)(2,1)S(1)}, s32[4,160]{1,0:T(4,128)S(1)}, f32[4,160]{1,0:T(4,128)S(1)}, bf16[128,2048]{1,0:T(8,128)(2,1)S(1)}, b...) custom-call(s32[4,160]{1,0:T(4,128)} %slots_hbm.1, f32[4,160]{1,0:T(4,128)} %gates_hbm.1, ...), custom_call_target="tpu_custom_call" | custom-call | tf_op jit(solution)/shard_map/pallas_call | solution.py:318
  2.2 14.3 %all_to_all.15.recv_ref = bf16[16,40,128]{2,1,0:T(8,128)(2,1)S(1)} all-to-all(bf16[16,40,128]{2,1,0:T(8,128)(2,1)S(1)} %get-tuple-element.28), channel_id=1, replica_groups=mesh['pair'=8,'odd'=2,'core'=2,'x'=4,'y'=4] {'x','y'}, dimensions={0} | all-to-all | bytes 327680 | tf_op jit(solution)/shard_map/all_to_all | solution.py:340
  16.5 1.1 shard_map.111
  17.6 5.0 %collective-permute-start = (f32[16,240,128]{2,1,0:T(8,128)S(1)}, f32[16,240,128]{2,1,0:T(8,128)S(1)}, u32[]{:S(2)}, u32[]{:S(2)}) collective-permute-start(f32[16,240,128]{2,1,0:T(8,128)S(1)} %get-tuple-element.35), channel_id=1, source_target_pairs={{0,16},{16,0},{1,17},{17,1},{2,18},{18,2},{3,19},{19,3},{4,20},{20... | collective-permute-start | bytes 5898248 | tf_op jit(solution)/shard_map/ppermute | solution.py:306
  22.6 3.6 %collective-permute-done.recv_ref = f32[16,240,128]{2,1,0:T(8,128)S(1)} collective-permute-done((f32[16,240,128]{2,1,0:T(8,128)S(1)}, f32[16,240,128]{2,1,0:T(8,128)S(1)}, u32[]{:S(2)}, u32[]{:S(2)}) %collective-permute-start) | collective-permute-done | bytes 1966112 | tf_op jit(solution)/shard_map/ppermute | solution.py:306
  26.2 0.3 shard_map.112
  26.5 2.5 %collective-permute-start.1 = (bf16[4,240,128]{2,1,0:T(8,128)(2,1)S(1)}, bf16[4,240,128]{2,1,0:T(8,128)(2,1)S(1)}, u32[]{:S(2)}, u32[]{:S(2)}) collective-permute-start(bf16[4,240,128]{2,1,0:T(8,128)(2,1)S(1)} %get-tuple-element.37), channel_id=1, source_target_pairs={{0,32},{32,64},{64,96},{96,128},{128,160},{160,192},{192,224},{224... | collective-permute-start | bytes 737288 | tf_op jit(solution)/shard_map/ppermute | solution.py:314
  29.0 9.5 %collective-permute-start.2 = (bf16[4,240,128]{2,1,0:T(8,128)(2,1)S(1)}, bf16[4,240,128]{2,1,0:T(8,128)(2,1)S(1)}, u32[]{:S(2)}, u32[]{:S(2)}) collective-permute-start(bf16[4,240,128]{2,1,0:T(8,128)(2,1)S(1)} %get-tuple-element.38), channel_id=1, source_target_pairs={{0,480},{32,0},{64,32},{96,64},{128,96},{160,128},{192,160},{224,1... | collective-permute-start | bytes 737288 | tf_op jit(solution)/shard_map/ppermute | solution.py:314
  38.5 4.0 %collective-permute-done.1.from_left_ref = bf16[4,240,128]{2,1,0:T(8,128)(2,1)S(1)} collective-permute-done((bf16[4,240,128]{2,1,0:T(8,128)(2,1)S(1)}, bf16[4,240,128]{2,1,0:T(8,128)(2,1)S(1)}, u32[]{:S(2)}, u32[]{:S(2)}) %collective-permute-start.1) | collective-permute-done | bytes 245792 | tf_op jit(solution)/shard_map/ppermute | solution.py:314
  42.5 0.9 collective-permute-done.2.from_right_ref
  43.4 0.1 shard_map.113
  43.5 30.2 %all_to_all.16.parts_ref = bf16[8,240,128]{2,1,0:T(8,128)(2,1)S(1)} all-to-all(bf16[8,240,128]{2,1,0:T(8,128)(2,1)S(1)} %get-tuple-element.39), channel_id=1, replica_groups=mesh['pair'=8,'odd'=2,'core'=2,'x'=4,'y'=4] {'pair'}, dimensions={0} | all-to-all | bytes 983040 | tf_op jit(solution)/shard_map/all_to_all | solution.py:360
  73.6 0.2 shard_map.114
  73.8 33.9 %all-gather = bf16[3968,128]{1,0:T(8,128)(2,1)S(1)} all-gather(bf16[248,128]{1,0:T(8,128)(2,1)S(1)} %shard_map.114), channel_id=2, replica_groups=mesh['pair'=8,'odd'=2,'core'=2,'x'=4,'y'=4] {'pair','odd'}, dimensions={0}, use_global_device_ids=true | all-gather | bytes 1079296 | tf_op jit(solution)/shard_map/all_gather | solution.py:362
  107.8 10.4 %collective-permute-start.3 = (bf16[16,248,128]{2,1,0:T(8,128)(2,1)S(1)}, bf16[16,248,128]{2,1,0:T(8,128)(2,1)S(1)}, u32[]{:S(2)}, u32[]{:S(2)}) collective-permute-start(bf16[16,248,128]{2,1,0:T(8,128)(2,1)S(1)} %bitcast.8), channel_id=1, source_target_pairs={{0,16},{16,0},{1,17},{17,1},{2,18},{18,2},{3,19},{19,3},{4,20},{20... | collective-permute-start | bytes 3047432 | tf_op jit(solution)/shard_map/ppermute | solution.py:306
  118.2 2.2 %collective-permute-done.3.other_ref = bf16[16,248,128]{2,1,0:T(8,128)(2,1)S(1)} collective-permute-done((bf16[16,248,128]{2,1,0:T(8,128)(2,1)S(1)}, bf16[16,248,128]{2,1,0:T(8,128)(2,1)S(1)}, u32[]{:S(2)}, u32[]{:S(2)}) %collective-permute-start.3) | collective-permute-done | bytes 1015840 | tf_op jit(solution)/shard_map/ppermute | solution.py:306
  120.4 2.2 %shard_map.115 = (bf16[128,2048]{1,0:T(8,128)(2,1)}, bf16[128,2048]{1,0:T(8,128)(2,1)}, bf16[2048,128]{1,0:T(8,128)(2,1)}, f32[16,24,128]{2,1,0:T(8,128)S(1)}) custom-call(s32[4,160]{1,0:T(4,128)S(1)} %get-tuple-element.26.slots_ref, bf16[160,128]{1,0:T(8,128)(2,1)S(1)} %get-tuple-element.32.inputs_ref, bf16[160,128]{1,0:T(8,128)(2,1)S(1)} %get-tuple-element.33.scaled_ref, ...), custom_call_target="tpu_custom_call" | custom-call | tf_op jit(solution)/shard_map/pallas_call | solution.py:284
  122.6 10.2 %all_to_all.17.incoming_ref = f32[16,24,128]{2,1,0:T(8,128)S(1)} all-to-all(f32[16,24,128]{2,1,0:T(8,128)S(1)} %get-tuple-element.41), channel_id=1, replica_groups=mesh['pair'=8,'odd'=2,'core'=2,'x'=4,'y'=4] {'x','y'}, dimensions={0} | all-to-all | bytes 393216 | tf_op jit(solution)/shard_map/all_to_all | solution.py:374
  132.8 1.6 %shard_map.116 = (bf16[320,128]{1,0:T(8,128)(2,1)}, f32[1,128]{1,0:T(1,128)}) custom-call(s32[4,160]{1,0:T(4,128)S(1)} %get-tuple-element.26.slots_ref, f32[16,24,128]{2,1,0:T(8,128)S(1)} %all_to_all.17.incoming_ref), custom_call_target="tpu_custom_call" | custom-call | tf_op jit(solution)/shard_map/pallas_call | solution.py:284
Async XLA Ops:
  17.6 8.6 %collective-permute-start = (f32[16,240,128]{2,1,0:T(8,128)S(1)}, f32[16,240,128]{2,1,0:T(8,128)S(1)}, u32[]{:S(2)}, u32[]{:S(2)}) collective-permute-start(f32[16,240,128]{2,1,0:T(8,128)S(1)} %get-tuple-element.35), channel_id=1, source_target_pairs={{0,16},{16,0},{1,17},{17,1},{2,18},{18,2},{3,19},{19,3},{4,20},{20... | collective-permute-start | bytes 5898248 | tf_op jit(solution)/shard_map/ppermute | solution.py:306
  26.5 16.0 %collective-permute-start.1 = (bf16[4,240,128]{2,1,0:T(8,128)(2,1)S(1)}, bf16[4,240,128]{2,1,0:T(8,128)(2,1)S(1)}, u32[]{:S(2)}, u32[]{:S(2)}) collective-permute-start(bf16[4,240,128]{2,1,0:T(8,128)(2,1)S(1)} %get-tuple-element.37), channel_id=1, source_target_pairs={{0,32},{32,64},{64,96},{96,128},{128,160},{160,192},{192,224},{224... | collective-permute-start | bytes 737288 | tf_op jit(solution)/shard_map/ppermute | solution.py:314
  29.0 14.4 %collective-permute-start.2 = (bf16[4,240,128]{2,1,0:T(8,128)(2,1)S(1)}, bf16[4,240,128]{2,1,0:T(8,128)(2,1)S(1)}, u32[]{:S(2)}, u32[]{:S(2)}) collective-permute-start(bf16[4,240,128]{2,1,0:T(8,128)(2,1)S(1)} %get-tuple-element.38), channel_id=1, source_target_pairs={{0,480},{32,0},{64,32},{96,64},{128,96},{160,128},{192,160},{224,1... | collective-permute-start | bytes 737288 | tf_op jit(solution)/shard_map/ppermute | solution.py:314
  107.8 12.6 %collective-permute-start.3 = (bf16[16,248,128]{2,1,0:T(8,128)(2,1)S(1)}, bf16[16,248,128]{2,1,0:T(8,128)(2,1)S(1)}, u32[]{:S(2)}, u32[]{:S(2)}) collective-permute-start(bf16[16,248,128]{2,1,0:T(8,128)(2,1)S(1)} %bitcast.8), channel_id=1, source_target_pairs={{0,16},{16,0},{1,17},{17,1},{2,18},{18,2},{3,19},{19,3},{4,20},{20... | collective-permute-start | bytes 3047432 | tf_op jit(solution)/shard_map/ppermute | solution.py:306

commit v4 on v3

--- a/solution.py
+++ b/solution.py
@@ -141,36 +141,25 @@
                 lanes = slice(LANES * side, LANES * side + LANES)
                 rows = slice(HALF * which, HALF * which + HALF)
                 keep_ref[2 * pair + side, rows, :] = total[:HALF, lanes]
-                send_ref[2 * pair + side, rows, :] = total[HALF:, lanes]
-
-
-def chip():
-    return 2 * lax.axis_index("pair") + lax.axis_index("odd")
-
-
-def pair_kernel(keep_ref, recv_ref, right_ref, left_ref, even_ref):
-    def both(distance):
-        block = lax.rem(chip() + distance + BLOCKS, BLOCKS)
-        return keep_ref[block] + recv_ref[block]
-
-    for step in range(4):
-        right_ref[step] = both(1 + 2 * step).astype(BF16)
-        left_ref[step] = both(-1 - 2 * step).astype(BF16)
-    for step in range(8):
-        even_ref[step] = both(2 * step)
-
-
-def near_kernel(even_ref, from_left_ref, from_right_ref, sums_ref, own_ref):
+                send_ref[2 * pair + side, rows, :] = total[HALF:, lanes].astype(BF16)
+
+
+def pair_kernel(keep_ref, recv_ref, give_ref, even_ref):
+    odd = lax.axis_index("odd")
+
+    def both(block):
+        return keep_ref[block] + recv_ref[block].astype(F32)
+
+    for pair in range(8):
+        give_ref[pair] = both(2 * pair + 1 - odd).astype(BF16)
+        even_ref[pair] = both(2 * pair + odd)
+
+
+def near_kernel(even_ref, recv_ref, sums_ref, own_ref):
     here = lax.axis_index("pair")
-    for step in range(8):
-        total = even_ref[step]
-        if step < 4:
-            total = total + from_left_ref[step].astype(F32)
-        if step == 0 or step > 4:
-            total = total + from_right_ref[(8 - step) % 8].astype(F32)
-        if step == 0:
-            own_ref[...] = total
-        sums_ref[lax.rem(here + step, 8)] = total.astype(BF16)
+    for pair in range(8):
+        sums_ref[pair] = (even_ref[pair] + recv_ref[pair].astype(F32)).astype(BF16)
+    own_ref[...] = even_ref[here] + recv_ref[here].astype(F32)
 
 
 def middle_kernel(gates_ref, parts_ref, own_ref, out_ref):
@@ -199,38 +188,32 @@
     out_ref[3 * HALF :, :] = tail.astype(BF16)
 
 
-def back_kernel(
-    slots_ref,
-    inputs_ref,
-    scaled_ref,
-    mine_ref,
-    other_ref,
-    gate_ref,
-    up_ref,
-    grad_gate_ref,
-    grad_up_ref,
-    grad_down_ref,
-    send_ref,
-):
-    core = lax.axis_index("core")
+def joined(mine_ref, other_ref, which, pair):
+    rows = slice(HALF * which, HALF * which + HALF)
+    sides = [
+        jnp.concatenate([mine_ref[place, rows, :], other_ref[place, rows, :]], axis=0)
+        for place in (2 * pair, 2 * pair + 1)
+    ]
+    return jnp.concatenate(sides, axis=1)
+
+
+def grads_kernel(inputs_ref, scaled_ref, mine_ref, other_ref, grad_gate_ref, grad_up_ref, grad_down_ref):
     inputs = inputs_ref[...]
     scaled = scaled_ref[...]
-
-    def joined(which, pair):
-        rows = slice(HALF * which, HALF * which + HALF)
-        sides = [
-            jnp.concatenate([mine_ref[place, rows, :], other_ref[place, rows, :]], axis=0)
-            for place in (2 * pair, 2 * pair + 1)
-        ]
-        return jnp.concatenate(sides, axis=1)
-
+    for pair in range(BLOCKS // 2):
+        cols = slice(256 * pair, 256 * pair + 256)
+        hidden, gate_side, up_side = (joined(mine_ref, other_ref, which, pair) for which in range(3))
+        grad_gate_ref[:, cols] = dot(inputs, gate_side, 0, 0).astype(BF16)
+        grad_up_ref[:, cols] = dot(inputs, up_side, 0, 0).astype(BF16)
+        grad_down_ref[cols, :] = dot(hidden, scaled, 0, 0).astype(BF16)
+
+
+def back_kernel(slots_ref, mine_ref, other_ref, gate_ref, up_ref, send_ref):
+    core = lax.axis_index("core")
     back = jnp.zeros((CAP, LANES), F32)
     for pair in range(BLOCKS // 2):
         cols = slice(256 * pair, 256 * pair + 256)
-        hidden, gate_side, up_side = joined(0, pair), joined(1, pair), joined(2, pair)
-        grad_gate_ref[:, cols] = dot(inputs, gate_side, 0, 0).astype(BF16)
-        grad_up_ref[:, cols] = dot(inputs, up_side, 0, 0).astype(BF16)
-        grad_down_ref[cols, :] = dot(hidden, scaled, 0, 0).astype(BF16)
+        gate_side, up_side = (joined(mine_ref, other_ref, which, pair) for which in (1, 2))
         back = back + dot(gate_side, gate_ref[:, cols], 1, 1) + dot(up_side, up_ref[:, cols], 1, 1)
 
     row = slots_ref[pl.ds(lax.axis_index("x"), 1), :]
@@ -310,8 +293,8 @@
     return pltpu.with_memory_space_constraint(value, pltpu.HBM)
 
 
-def shift(value, step):
-    return lax.ppermute(value, Z, [(z, (z + step) % BLOCKS) for z in range(BLOCKS)])
+def swap_chips(value):
+    return lax.ppermute(value, Z, [(z, z ^ 1) for z in range(BLOCKS)])
 
 
 def per_device(tokens, out_grad, slot_tokens, slot_gate, w_gate, w_up, w_down):
@@ -338,38 +321,36 @@
         near(value) for value in (slots, gates, gate_weight, up_weight, down_weight)
     )
     recv = lax.all_to_all(send, ("x", "y"), split_axis=0, concat_axis=0, tiled=True)
-    halves = on_chip((BLOCKS, 3 * HALF, LANES), F32)
+    halves = (BLOCKS, 3 * HALF, LANES)
     rows = on_chip((CAP, LANES), BF16)
     keep, give, inputs, scaled = call(
         front_kernel,
-        (halves, halves, rows, rows),
+        (on_chip(halves, F32), on_chip(halves, BF16), rows, rows),
         (slots, gates, near(recv), gate_weight, up_weight, down_weight),
     )
-    quarter = on_chip((4, 3 * HALF, LANES), BF16)
-    right, left, even = call(
-        pair_kernel,
-        (quarter, quarter, on_chip((8, 3 * HALF, LANES), F32)),
-        (near(keep), near(swap_cores(give))),
-    )
-    from_left, from_right = shift(right, 1), shift(left, -1)
+    part = (8, 3 * HALF, LANES)
+    give, even = call(
+        pair_kernel, (on_chip(part, BF16), on_chip(part, F32)), (near(keep), near(swap_cores(give)))
+    )
     sums, own = call(
         near_kernel,
-        (on_chip((8, 3 * HALF, LANES), BF16), on_chip((3 * HALF, LANES), F32)),
-        (near(even), near(from_left), near(from_right)),
+        (on_chip(part, BF16), on_chip((3 * HALF, LANES), F32)),
+        (near(even), near(swap_chips(give))),
     )
     parts = lax.all_to_all(sums, "pair", split_axis=0, concat_axis=0, tiled=True)
     piece = call(middle_kernel, on_chip((PIECE, LANES), BF16), (gates, near(parts), near(own)))
     mine = lax.all_gather(piece, Z, axis=0, tiled=False)
     other = swap_cores(mine)
-    grad_gate, grad_up, grad_down, outgoing = call(
+    mine, other = near(mine), near(other)
+    outgoing = call(
         back_kernel,
-        (
-            shape(gate_weight.shape, BF16),
-            shape(up_weight.shape, BF16),
-            shape(down_weight.shape, BF16),
-            on_chip((OWNERS, ROOM, LANES), F32),
-        ),
-        (slots, near(inputs), near(scaled), near(mine), near(other), gate_weight, up_weight),
+        on_chip((OWNERS, ROOM, LANES), F32),
+        (slots, mine, other, gate_weight, up_weight),
+    )
+    grad_gate, grad_up, grad_down = call(
+        grads_kernel,
+        (shape(gate_weight.shape, BF16), shape(up_weight.shape, BF16), shape(down_weight.shape, BF16)),
+        (near(inputs), near(scaled), mine, other),
     )
     incoming = lax.all_to_all(outgoing, ("x", "y"), split_axis=0, concat_axis=0, tiled=True)
     grad_tokens, gate_line = call(

time: 135 us -> 136 us (level)
  waiting for transfers between devices: 10.7 us -> 21.3 us
  starting transfers between devices: 27.4 us -> 21 us
  blocking collectives: 88.6 us -> 83.3 us
  Pallas kernels: 7 us -> 9.17 us
    all_to_all x1 -> x0, blocking collectives: 10.2 us -> none  [per_device(): lax.all_to_all(outgoing, ('x', 'y'), split_axis=0, concat_axis=0, tiled=T...]
    ppermute x2 -> x1, starting transfers between devices: 12 us -> 2.47 us  [swap_chips(): return lax.ppermute(value, Z, [(z, z ^ 1) for z in range(BLOCKS)])]
    all_to_all x1, blocking collectives: 30.2 us -> 37.4 us  [per_device(): lax.all_to_all(sums, 'pair', split_axis=0, concat_axis=0, tiled=True)]
    ppermute x2 -> x1, waiting for transfers between devices: 4.92 us -> 11.8 us  [swap_chips(): return lax.ppermute(value, Z, [(z, z ^ 1) for z in range(BLOCKS)])]
    all_to_all x0 -> x1, waiting for transfers between devices: none -> 5.08 us  [per_device(): lax.all_to_all(outgoing, ('x', 'y'), split_axis=0, concat_axis=0, tiled=T...]
    all_to_all x0 -> x1, starting transfers between devices: none -> 3.52 us  [per_device(): lax.all_to_all(outgoing, ('x', 'y'), split_axis=0, concat_axis=0, tiled=T...]
    all_gather x1, blocking collectives: 33.9 us -> 31.6 us  [per_device(): mine = lax.all_gather(piece, Z, axis=0, tiled=False)]
    pallas_call x6 -> x7, Pallas kernels: 5.47 us -> 7.63 us  [call(): pl.pallas_call(kernel, out_shape=out_shape, in_specs=[VMEM] * len(inputs)...]
  transfers between devices with their start and end apart: 4 -> 4, of which waited for: 4 -> 4; matrix products, arithmetic and copies ran while one was open for 0% -> 0% of each run, Pallas kernels for 0% -> 1%
where the time goes in v4:
time: 136 us; the launch traced here: 135 us
  blocking collectives  83.3 us (61%)
  waiting for transfers between devices  21.3 us (16%)
  starting transfers between devices  21 us (15%)
  Pallas kernels  9.17 us (7%)
    all_to_all x1, blocking collectives, per_device(): lax.all_to_all(sums, 'pair', split_axis=0, concat_axis=0, tiled=True)  37.4 us
    all_gather x1, blocking collectives, per_device(): mine = lax.all_gather(piece, Z, axis=0, tiled=False)  31.6 us
    ppermute x2, starting transfers between devices, swap_cores(): return lax.ppermute(value, 'core', [(0, 1), (1, 0)])  15 us
    all_to_all x1, blocking collectives, per_device(): lax.all_to_all(send, ('x', 'y'), split_axis=0, concat_axis=0, tiled=True)  14.3 us
    ppermute x1, waiting for transfers between devices, swap_chips(): return lax.ppermute(value, Z, [(z, z ^ 1) for z in range(BLOCKS)])  11.8 us
    pallas_call x7, Pallas kernels, call(): pl.pallas_call(kernel, out_shape=out_shape, in_specs=[VMEM] * len(inputs)...  7.63 us
    all_to_all x1, waiting for transfers between devices, per_device(): lax.all_to_all(outgoing, ('x', 'y'), split_axis=0, concat_axis=0, tiled=T...  5.08 us
    ppermute x2, waiting for transfers between devices, swap_cores(): return lax.ppermute(value, 'core', [(0, 1), (1, 0)])  4.39 us
  transfers between devices with their start and end apart: 4, of which 4 were waited for; matrix products, arithmetic and copies ran while one was open for 0% of the time, Pallas kernels for 1%

profile of v4, /device:TPU:1, one launch (start us, length us, event | category | flops | bytes accessed | tf_op | source)
XLA Modules:
  0.0 135.4 jit_solution(6902785893768743)
XLA Ops:
  0.6 1.5 %shard_map.110 = (bf16[16,40,128]{2,1,0:T(8,128)(2,1)S(1)}, s32[4,160]{1,0:T(4,128)S(1)}, f32[4,160]{1,0:T(4,128)S(1)}, bf16[128,2048]{1,0:T(8,128)(2,1)S(1)}, b...) custom-call(s32[4,160]{1,0:T(4,128)} %slots_hbm.1, f32[4,160]{1,0:T(4,128)} %gates_hbm.1, ...), custom_call_target="tpu_custom_call" | custom-call | tf_op jit(solution)/shard_map/pallas_call | solution.py:301
  2.2 14.3 %all_to_all.15.recv_ref = bf16[16,40,128]{2,1,0:T(8,128)(2,1)S(1)} all-to-all(bf16[16,40,128]{2,1,0:T(8,128)(2,1)S(1)} %get-tuple-element.26), channel_id=1, replica_groups=mesh['pair'=8,'odd'=2,'core'=2,'x'=4,'y'=4] {'x','y'}, dimensions={0} | all-to-all | bytes 327680 | tf_op jit(solution)/shard_map/all_to_all | solution.py:323
  16.5 1.1 shard_map.111
  17.6 5.0 %collective-permute-start = (bf16[16,240,128]{2,1,0:T(8,128)(2,1)S(1)}, bf16[16,240,128]{2,1,0:T(8,128)(2,1)S(1)}, u32[]{:S(2)}, u32[]{:S(2)}) collective-permute-start(bf16[16,240,128]{2,1,0:T(8,128)(2,1)S(1)} %get-tuple-element.31), channel_id=1, source_target_pairs={{0,16},{16,0},{1,17},{17,1},{2,18},{18,2},{3,19},{19,3},{4,20},{20... | collective-permute-start | bytes 2949128 | tf_op jit(solution)/shard_map/ppermute | solution.py:289
  22.6 2.2 %collective-permute-done.recv_ref = bf16[16,240,128]{2,1,0:T(8,128)(2,1)S(1)} collective-permute-done((bf16[16,240,128]{2,1,0:T(8,128)(2,1)S(1)}, bf16[16,240,128]{2,1,0:T(8,128)(2,1)S(1)}, u32[]{:S(2)}, u32[]{:S(2)}) %collective-permute-start) | collective-permute-done | bytes 983072 | tf_op jit(solution)/shard_map/ppermute | solution.py:289
  24.8 0.2 shard_map.112
  25.0 2.5 %collective-permute-start.1 = (bf16[8,240,128]{2,1,0:T(8,128)(2,1)S(1)}, bf16[8,240,128]{2,1,0:T(8,128)(2,1)S(1)}, u32[]{:S(2)}, u32[]{:S(2)}) collective-permute-start(bf16[8,240,128]{2,1,0:T(8,128)(2,1)S(1)} %get-tuple-element.33), channel_id=1, source_target_pairs={{0,32},{32,0},{64,96},{96,64},{128,160},{160,128},{192,224},{224,1... | collective-permute-start | bytes 1474568 | tf_op jit(solution)/shard_map/ppermute | solution.py:297
  27.5 11.8 %collective-permute-done.1.recv_ref = bf16[8,240,128]{2,1,0:T(8,128)(2,1)S(1)} collective-permute-done((bf16[8,240,128]{2,1,0:T(8,128)(2,1)S(1)}, bf16[8,240,128]{2,1,0:T(8,128)(2,1)S(1)}, u32[]{:S(2)}, u32[]{:S(2)}) %collective-permute-start.1) | collective-permute-done | bytes 491552 | tf_op jit(solution)/shard_map/ppermute | solution.py:297
  39.3 0.1 shard_map.113
  39.4 37.4 %all_to_all.16.parts_ref = bf16[8,240,128]{2,1,0:T(8,128)(2,1)S(1)} all-to-all(bf16[8,240,128]{2,1,0:T(8,128)(2,1)S(1)} %get-tuple-element.34), channel_id=1, replica_groups=mesh['pair'=8,'odd'=2,'core'=2,'x'=4,'y'=4] {'pair'}, dimensions={0} | all-to-all | bytes 983040 | tf_op jit(solution)/shard_map/all_to_all | solution.py:340
  76.8 0.2 shard_map.114
  77.0 31.6 %all-gather = bf16[3968,128]{1,0:T(8,128)(2,1)S(1)} all-gather(bf16[248,128]{1,0:T(8,128)(2,1)S(1)} %shard_map.114), channel_id=2, replica_groups=mesh['pair'=8,'odd'=2,'core'=2,'x'=4,'y'=4] {'pair','odd'}, dimensions={0}, use_global_device_ids=true | all-gather | bytes 1079296 | tf_op jit(solution)/shard_map/all_gather | solution.py:342
  108.6 10.0 %collective-permute-start.2 = (bf16[16,248,128]{2,1,0:T(8,128)(2,1)S(1)}, bf16[16,248,128]{2,1,0:T(8,128)(2,1)S(1)}, u32[]{:S(2)}, u32[]{:S(2)}) collective-permute-start(bf16[16,248,128]{2,1,0:T(8,128)(2,1)S(1)} %bitcast.8), channel_id=1, source_target_pairs={{0,16},{16,0},{1,17},{17,1},{2,18},{18,2},{3,19},{19,3},{4,20},{20... | collective-permute-start | bytes 3047432 | tf_op jit(solution)/shard_map/ppermute | solution.py:289
  118.6 2.2 %collective-permute-done.2.other_ref = bf16[16,248,128]{2,1,0:T(8,128)(2,1)S(1)} collective-permute-done((bf16[16,248,128]{2,1,0:T(8,128)(2,1)S(1)}, bf16[16,248,128]{2,1,0:T(8,128)(2,1)S(1)}, u32[]{:S(2)}, u32[]{:S(2)}) %collective-permute-start.2) | collective-permute-done | bytes 1015840 | tf_op jit(solution)/shard_map/ppermute | solution.py:289
  120.8 2.6 %shard_map.115 = f32[16,24,128]{2,1,0:T(8,128)} custom-call(s32[4,160]{1,0:T(4,128)S(1)} %get-tuple-element.24.slots_ref, bf16[16,248,128]{2,1,0:T(8,128)(2,1)S(1)} %bitcast.9, bf16[16,248,128]{2,1,0:T(8,128)(2,1)S(1)} %collective-permute-done.2.other_ref, bf16[128,2048]{1,0:T(8,128)(2,1)S(1)} %get-tuple-element.27.gate_ref, ...), custom_call_target="tpu_custom_call" | custom-call | tf_op jit(solution)/shard_map/pallas_call | solution.py:267
  123.4 3.5 %all-to-all-start.2 = ((f32[16,24,128]{2,1,0:T(8,128)}), f32[16,24,128]{2,1,0:T(8,128)S(1)}, u32[]{:S(2)}, u32[]{:S(2)}) async-start(f32[16,24,128]{2,1,0:T(8,128)} %shard_map.115), calls=%async_computation.2 | async-start | bytes 393216 | tf_op jit(solution)/shard_map/all_to_all | solution.py:355
  126.9 1.8 %shard_map.117 = (bf16[128,2048]{1,0:T(8,128)(2,1)}, bf16[128,2048]{1,0:T(8,128)(2,1)}, bf16[2048,128]{1,0:T(8,128)(2,1)}) custom-call(bf16[160,128]{1,0:T(8,128)(2,1)S(1)} %get-tuple-element.37.inputs_ref, bf16[160,128]{1,0:T(8,128)(2,1)S(1)} %get-tuple-element.38.scaled_ref, bf16[16,248,128]{2,1,0:T(8,128)(2,1)S(1)} %bitcast.10, ...), custom_call_target="tpu_custom_call" | custom-call | tf_op jit(solution)/shard_map/pallas_call | solution.py:267
  128.8 5.1 %all-to-all-done.2.incoming_ref = f32[16,24,128]{2,1,0:T(8,128)S(1)} async-done(((f32[16,24,128]{2,1,0:T(8,128)}), f32[16,24,128]{2,1,0:T(8,128)S(1)}, u32[]{:S(2)}, u32[]{:S(2)}) %all-to-all-start.2) | async-done | bytes 196640 | tf_op jit(solution)/shard_map/all_to_all | solution.py:355
  133.8 1.6 %shard_map.116 = (bf16[320,128]{1,0:T(8,128)(2,1)}, f32[1,128]{1,0:T(1,128)}) custom-call(s32[4,160]{1,0:T(4,128)S(1)} %get-tuple-element.24.slots_ref, f32[16,24,128]{2,1,0:T(8,128)S(1)} %all-to-all-done.2.incoming_ref), custom_call_target="tpu_custom_call" | custom-call | tf_op jit(solution)/shard_map/pallas_call | solution.py:267
Async XLA Ops:
  17.6 7.2 %collective-permute-start = (bf16[16,240,128]{2,1,0:T(8,128)(2,1)S(1)}, bf16[16,240,128]{2,1,0:T(8,128)(2,1)S(1)}, u32[]{:S(2)}, u32[]{:S(2)}) collective-permute-start(bf16[16,240,128]{2,1,0:T(8,128)(2,1)S(1)} %get-tuple-element.31), channel_id=1, source_target_pairs={{0,16},{16,0},{1,17},{17,1},{2,18},{18,2},{3,19},{19,3},{4,20},{20... | collective-permute-start | bytes 2949128 | tf_op jit(solution)/shard_map/ppermute | solution.py:289
  25.0 14.3 %collective-permute-start.1 = (bf16[8,240,128]{2,1,0:T(8,128)(2,1)S(1)}, bf16[8,240,128]{2,1,0:T(8,128)(2,1)S(1)}, u32[]{:S(2)}, u32[]{:S(2)}) collective-permute-start(bf16[8,240,128]{2,1,0:T(8,128)(2,1)S(1)} %get-tuple-element.33), channel_id=1, source_target_pairs={{0,32},{32,0},{64,96},{96,64},{128,160},{160,128},{192,224},{224,1... | collective-permute-start | bytes 1474568 | tf_op jit(solution)/shard_map/ppermute | solution.py:297
  108.6 12.2 %collective-permute-start.2 = (bf16[16,248,128]{2,1,0:T(8,128)(2,1)S(1)}, bf16[16,248,128]{2,1,0:T(8,128)(2,1)S(1)}, u32[]{:S(2)}, u32[]{:S(2)}) collective-permute-start(bf16[16,248,128]{2,1,0:T(8,128)(2,1)S(1)} %bitcast.8), channel_id=1, source_target_pairs={{0,16},{16,0},{1,17},{17,1},{2,18},{18,2},{3,19},{19,3},{4,20},{20... | collective-permute-start | bytes 3047432 | tf_op jit(solution)/shard_map/ppermute | solution.py:289
  123.4 10.4 %all-to-all-start.2 = ((f32[16,24,128]{2,1,0:T(8,128)}), f32[16,24,128]{2,1,0:T(8,128)S(1)}, u32[]{:S(2)}, u32[]{:S(2)}) async-start(f32[16,24,128]{2,1,0:T(8,128)} %shard_map.115), calls=%async_computation.2 | async-start | bytes 393216 | tf_op jit(solution)/shard_map/all_to_all | solution.py:355

commit v5 on v3

v5 whole, which is shorter than its diff:
```python
import jax
import jax.numpy as jnp
from jax import lax
from jax.experimental import pallas as pl
from jax.experimental.pallas import tpu as pltpu
from jax.sharding import Mesh
from jax.sharding import PartitionSpec as P

BF16 = jnp.bfloat16
F32 = jnp.float32
I32 = jnp.int32

TOK = 320
CAP = 160
HALF = 80
OWNERS = 16
FLIGHT = 4
MOST = 20
ROOM = 24
LANES = 128
CHIPS = 16
BLOCKS = 8
PIECE = 3 * HALF + 8

Z = ("pair", "odd")
VMEM = pl.BlockSpec(memory_space=pltpu.VMEM)


def iota(shape, dim):
    return lax.broadcasted_iota(I32, shape, dim)


def dot(left, right, left_dim=1, right_dim=0, precision=None):
    return lax.dot_general(
        left,
        right,
        (((left_dim,), (right_dim,)), ((), ())),
        preferred_element_type=F32,
        precision=precision,
    )


def owned_tokens(row, first, rows, room):
    start = jnp.sum((row < first).astype(I32), axis=1, keepdims=True)
    count = jnp.sum(((row >= first) & (row < first + TOK)).astype(I32), axis=1, keepdims=True)
    rank = lax.rem(iota((rows, CAP), 0), room)
    chosen = (iota((rows, CAP), 1) == start + rank) & (rank < count)
    token = jnp.sum(jnp.where(chosen, row - first + 1, 0), axis=1, keepdims=True)
    return token - 1


def column(row, odd):
    slot = lax.rem(iota((CAP, CAP), 0) + HALF * odd, CAP)
    return jnp.sum(jnp.where(iota((CAP, CAP), 1) == slot, row, 0), axis=1, keepdims=True)


def places(row, odd):
    token = column(row, odd)
    owner = jnp.sum(
        ((iota((CAP, LANES), 1) < OWNERS - 1) & (token >= TOK * (iota((CAP, LANES), 1) + 1))).astype(I32),
        axis=1,
        keepdims=True,
    )
    start = jnp.sum((row < TOK * owner).astype(I32), axis=1, keepdims=True)
    slot = lax.rem(iota((CAP, 1), 0) + HALF * odd, CAP)
    return owner, slot - start


def block_of(core, block):
    return pl.ds(pl.multiple_of((BLOCKS * core + block) * LANES, LANES), LANES)


def dispatch_kernel(
    slots_hbm,
    gates_hbm,
    tokens_hbm,
    grads_hbm,
    gate_hbm,
    up_hbm,
    down_hbm,
    send_ref,
    slots_ref,
    gates_ref,
    have_ref,
    give_ref,
    tokens_ref,
    grads_ref,
    sems,
):
    core = lax.axis_index("core")
    pairs = [
        (slots_hbm, slots_ref),
        (tokens_hbm, tokens_ref),
        (grads_hbm, grads_ref),
        (gates_hbm, gates_ref),
    ]
    for side, target in ((1 - core, give_ref), (core, have_ref)):
        for block in range(BLOCKS):
            pairs.append((gate_hbm.at[:, block_of(side, block)], target.at[0, block]))
            pairs.append((up_hbm.at[:, block_of(side, block)], target.at[1, block]))
            pairs.append((down_hbm.at[block_of(side, block), :], target.at[2, block]))
    copies = [pltpu.make_async_copy(source, target, sems.at[i]) for i, (source, target) in enumerate(pairs)]
    for copy in copies:
        copy.start()
    for copy in copies[:3]:
        copy.wait()
    first = TOK * (4 * lax.axis_index("x") + lax.axis_index("y"))
    rows = 2 * MOST
    for expert in range(FLIGHT):
        local = owned_tokens(slots_ref[expert : expert + 1, :], first, rows, MOST)
        hit = local == iota((rows, TOK), 1)
        upper = iota((rows, TOK), 0) < MOST
        pick_tokens = jnp.where(hit & upper, 1.0, 0.0).astype(BF16)
        pick_grads = jnp.where(hit & ~upper, 1.0, 0.0).astype(BF16)
        rows_out = (dot(pick_tokens, tokens_ref[...]) + dot(pick_grads, grads_ref[...])).astype(BF16)
        for side in range(2):
            for part in range(4):
                send_ref[OWNERS * side + 4 * expert + part] = rows_out
    for copy in copies[3:]:
        copy.wait()


def tile(have_ref, other_ref, which, blocks):
    axis = 1 if which == 2 else 0
    return jnp.concatenate(
        [
            jnp.concatenate([ref[which, block] for block in blocks], axis=1 - axis)
            for ref in (have_ref, other_ref)
        ],
        axis=axis,
    )


def front_kernel(
    slots_ref, gates_ref, recv_ref, have_ref, other_ref, even_ref, right_ref, left_ref, inputs_ref, scaled_ref
):
    expert = lax.axis_index("x")
    core = lax.axis_index("core")
    odd = lax.axis_index("odd")
    row = slots_ref[pl.ds(expert, 1), :]
    owner, rank = places(row, odd)
    place = owner * (2 * MOST) + rank
    width = OWNERS * 2 * MOST
    where = iota((CAP, width), 1)
    pick_inputs = jnp.where(where == place, 1.0, 0.0).astype(BF16)
    pick_grads = jnp.where(where == place + MOST, 1.0, 0.0).astype(BF16)
    gates = column(gates_ref[pl.ds(expert, 1), :], odd)
    for index, side in enumerate((core, 1 - core)):
        recv = recv_ref[pl.ds(OWNERS * side, OWNERS)].reshape(width, LANES)
        lanes = slice(LANES * index, LANES * index + LANES)
        inputs_ref[:, lanes] = dot(pick_inputs, recv).astype(BF16)
        scaled_ref[:, lanes] = (gates * dot(pick_grads, recv)).astype(BF16)
    inputs = inputs_ref[...]
    scaled = scaled_ref[...]
    for pair in range(BLOCKS // 2):
        steps = (2 * pair, 2 * pair + 1)
        blocks = [lax.rem(lax.axis_index("pair") + odd + step, BLOCKS) for step in steps]
        sums = (
            dot(inputs, tile(have_ref, other_ref, 0, blocks)),
            dot(inputs, tile(have_ref, other_ref, 1, blocks)),
            dot(scaled, tile(have_ref, other_ref, 2, blocks), 1, 1),
        )
        give_ref = right_ref if pair < 2 else left_ref
        for which, total in enumerate(sums):
            rows = slice(HALF * which, HALF * which + HALF)
            for side in range(2):
                lanes = slice(LANES * side, LANES * side + LANES)
                even_ref[blocks[side], rows, :] = total[:HALF, lanes]
                give_ref[steps[side] % 4, rows, :] = total[HALF:, lanes].astype(BF16)


def near_kernel(even_ref, from_left_ref, from_right_ref, sums_ref, own_ref):
    here = lax.axis_index("pair")
    for step in range(BLOCKS):
        block = lax.rem(here + step, BLOCKS)
        total = even_ref[block]
        if step < 4:
            total = total + from_left_ref[step].astype(F32)
        if step == 0 or step > 4:
            total = total + from_right_ref[3 - (BLOCKS - step) % BLOCKS].astype(F32)
        if step == 0:
            own_ref[...] = total
        sums_ref[block] = total.astype(BF16)


def middle_kernel(gates_ref, parts_ref, own_ref, out_ref):
    gates = column(gates_ref[pl.ds(lax.axis_index("x"), 1), :], lax.axis_index("odd"))[:HALF]

    def total(which):
        rows = slice(HALF * which, HALF * which + HALF)
        result = own_ref[rows, :]
        for step in range(1, BLOCKS):
            result = result + parts_ref[lax.rem(lax.axis_index("pair") + step, BLOCKS), rows, :].astype(F32)
        return result

    pre_gate, pre_up, upstream = total(0), total(1), total(2)
    sigmoid = jax.nn.sigmoid(pre_gate)
    hidden = (pre_gate * sigmoid * pre_up).astype(BF16)
    out_ref[:HALF, :] = hidden
    out_ref[HALF : 2 * HALF, :] = (upstream * pre_up * sigmoid * (1.0 + pre_gate * (1.0 - sigmoid))).astype(BF16)
    out_ref[2 * HALF : 3 * HALF, :] = (upstream * pre_gate * sigmoid).astype(BF16)
    part = jnp.sum(hidden.astype(F32) * upstream, axis=1, keepdims=True) / gates
    eye = iota((HALF, LANES), 0) == iota((HALF, LANES), 1)
    part = jnp.sum(jnp.where(eye, part, 0.0), axis=0, keepdims=True)
    high = part.astype(BF16).astype(F32)
    line = iota((8, LANES), 0)
    tail = jnp.where(line == 0, high, jnp.where(line == 1, part - high, 0.0))
    out_ref[3 * HALF :, :] = tail.astype(BF16)


def back_kernel(
    slots_ref, inputs_ref, scaled_ref, parts_ref, have_ref, other_ref, own_ref, give_ref, send_ref
):
    core = lax.axis_index("core")
    odd = lax.axis_index("odd")
    inputs = inputs_ref[...]
    scaled = scaled_ref[...]

    def joined(which, blocks):
        rows = slice(HALF * which, HALF * which + HALF)
        return jnp.concatenate(
            [
                jnp.concatenate([parts_ref[2 * block + half, rows, :] for half in (odd, 1 - odd)], axis=0)
                for block in blocks
            ],
            axis=1,
        )

    first, second = slice(0, LANES), slice(LANES, 2 * LANES)
    back = jnp.zeros((CAP, 2 * LANES), F32)
    for pair in range(BLOCKS // 2):
        blocks = (2 * pair, 2 * pair + 1)
        hidden, gate_side, up_side = joined(0, blocks), joined(1, blocks), joined(2, blocks)
        for which, side in ((0, gate_side), (1, up_side)):
            grad = dot(inputs, side, 0, 0).astype(BF16)
            for block, cols in zip(blocks, (first, second)):
                own_ref[which, block] = grad[first, cols]
                give_ref[which, block] = grad[second, cols]
            back = back + dot(side, tile(have_ref, other_ref, which, blocks), 1, 1)
        grad = dot(hidden, scaled, 0, 0).astype(BF16)
        for block, rows in zip(blocks, (first, second)):
            own_ref[2, block] = grad[rows, first]
            give_ref[2, block] = grad[rows, second]

    row = slots_ref[pl.ds(lax.axis_index("x"), 1), :]
    owner, rank = places(row, odd)
    spread = jnp.where(iota((CAP, OWNERS * ROOM), 1) == owner * ROOM + rank, 1.0, 0.0)
    buckets = dot(spread, back, 0, 0, lax.Precision.HIGHEST)

    def gate_row(half):
        lines = jnp.zeros((8, LANES), F32)
        for block in range(BLOCKS):
            lines = lines + parts_ref[2 * block + half, 3 * HALF :, :].astype(F32)
        return jnp.broadcast_to(jnp.sum(lines, axis=0, keepdims=True), (8, LANES))

    halves = [gate_row(half) for half in range(2)]
    line = iota((8, LANES), 0)
    for quarter in range(4):
        slot = iota((LANES, LANES), 1) + 40 * quarter
        valid = iota((LANES, LANES), 1) < 40
        gates = jnp.zeros((8, LANES), F32)
        for half in range(2):
            take = jnp.where(valid & (iota((LANES, LANES), 0) + HALF * half == slot), 1.0, 0.0)
            take = jnp.where(iota((LANES, LANES), 0) < HALF, take, 0.0)
            gates = gates + dot(halves[half], take, precision=lax.Precision.HIGHEST)
        for expert in range(FLIGHT):
            place = 4 * expert + quarter
            for side, lanes in ((core, first), (1 - core, second)):
                bucket = buckets[ROOM * place : ROOM * place + ROOM, lanes]
                send_ref[OWNERS * side + place, :16, :] = bucket[:16]
                send_ref[OWNERS * side + place, 16:, :] = jnp.where(line == 4, gates, bucket[16:])


def last_kernel(
    slots_ref,
    incoming_ref,
    own_ref,
    other_ref,
    tokens_ref,
    gates_ref,
    grad_gate_hbm,
    grad_up_hbm,
    grad_down_hbm,
    sems,
):
    core = lax.axis_index("core")
    pairs = []
    for side, source in ((core, own_ref), (1 - core, other_ref)):
        for block in range(BLOCKS):
            pairs.append((source.at[0, block], grad_gate_hbm.at[:, block_of(side, block)]))
            pairs.append((source.at[1, block], grad_up_hbm.at[:, block_of(side, block)]))
            pairs.append((source.at[2, block], grad_down_hbm.at[block_of(side, block), :]))
    copies = [pltpu.make_async_copy(source, target, sems.at[i]) for i, (source, target) in enumerate(pairs)]
    for copy in copies:
        copy.start()

    def arrived(expert, rows):
        parts = [incoming_ref[OWNERS * side + 4 * expert + part, rows, :] for side in range(2) for part in range(4)]
        total = parts[0]
        for part in parts[1:]:
            total = total + part
        return total

    expert_here = lax.axis_index("x")
    first = TOK * (4 * expert_here + lax.axis_index("y"))
    total = jnp.zeros((TOK, LANES), F32)
    for expert in range(FLIGHT):
        local = owned_tokens(slots_ref[expert : expert + 1, :], first, ROOM, ROOM)
        pick = jnp.where(local == iota((ROOM, TOK), 1), 1.0, 0.0)
        total = total + dot(pick, arrived(expert, slice(0, ROOM)), 0, 0, lax.Precision.HIGHEST)
    tokens_ref[...] = total.astype(BF16)
    gates_ref[...] = arrived(expert_here, slice(16, ROOM))[4:5, :]
    for copy in copies:
        copy.wait()


def call(kernel, out_shape, inputs):
    return pl.pallas_call(
        kernel,
        out_shape=out_shape,
        in_specs=[VMEM] * len(inputs),
        out_specs=jax.tree.map(lambda _: VMEM, out_shape),
        compiler_params=pltpu.CompilerParams(vmem_limit_bytes=24 << 20),
    )(*inputs)


def shape(dims, kind):
    return jax.ShapeDtypeStruct(dims, kind)


def on_chip(dims, kind):
    return pltpu.VMEM(dims, kind)


def near(value):
    return pltpu.with_memory_space_constraint(value, pltpu.VMEM)


def swap_cores(value):
    return lax.ppermute(value, "core", [(0, 1), (1, 0)])


def far(value):
    return pltpu.with_memory_space_constraint(value, pltpu.HBM)


def shift(value, step):
    return lax.ppermute(value, Z, [(z, (z + step) % CHIPS) for z in range(CHIPS)])


def per_device(tokens, out_grad, slot_tokens, slot_gate, w_gate, w_up, w_down):
    weights = (3, BLOCKS, LANES, LANES)
    send, slots, gates, have, give = pl.pallas_call(
        dispatch_kernel,
        out_shape=(
            on_chip((2 * OWNERS, 2 * MOST, LANES), BF16),
            on_chip(slot_tokens.shape, I32),
            on_chip(slot_gate.shape, F32),
            on_chip(weights, BF16),
            on_chip(weights, BF16),
        ),
        in_specs=[pl.BlockSpec(memory_space=pltpu.HBM)] * 7,
        out_specs=(VMEM,) * 5,
        scratch_shapes=[
            pltpu.VMEM(tokens.shape, BF16),
            pltpu.VMEM(tokens.shape, BF16),
            pltpu.SemaphoreType.DMA((4 + 6 * BLOCKS,)),
        ],
        compiler_params=pltpu.CompilerParams(vmem_limit_bytes=24 << 20),
    )(*(far(value) for value in (slot_tokens, slot_gate, tokens, out_grad, w_gate[0], w_up[0], w_down[0])))
    slots, gates, have, other = near(slots), near(gates), near(have), near(swap_cores(give))
    everyone = ("core", "x", "y")
    recv = lax.all_to_all(send, everyone, split_axis=0, concat_axis=0, tiled=True)
    part = (BLOCKS, 3 * HALF, LANES)
    quarter = on_chip((4, 3 * HALF, LANES), BF16)
    rows = on_chip((CAP, 2 * LANES), BF16)
    even, right, left, inputs, scaled = call(
        front_kernel,
        (on_chip(part, F32), quarter, quarter, rows, rows),
        (slots, gates, near(recv), have, other),
    )
    from_left, from_right = shift(right, 1), shift(left, -1)
    sums, own = call(
        near_kernel,
        (on_chip(part, BF16), on_chip((3 * HALF, LANES), F32)),
        (near(even), near(from_left), near(from_right)),
    )
    parts = lax.all_to_all(sums, "pair", split_axis=0, concat_axis=0, tiled=True)
    piece = call(middle_kernel, on_chip((PIECE, LANES), BF16), (gates, near(parts), near(own)))
    pieces = lax.all_gather(piece, Z, axis=0, tiled=False)
    mine, give, outgoing = call(
        back_kernel,
        (on_chip(weights, BF16), on_chip(weights, BF16), on_chip((2 * OWNERS, ROOM, LANES), F32)),
        (slots, near(inputs), near(scaled), near(pieces), have, other),
    )
    incoming = lax.all_to_all(outgoing, everyone, split_axis=0, concat_axis=0, tiled=True)
    grad_tokens, gate_line, grad_gate, grad_up, grad_down = pl.pallas_call(
        last_kernel,
        out_shape=(
            shape((TOK, LANES), BF16),
            shape((1, LANES), F32),
            shape(w_gate.shape[1:], BF16),
            shape(w_up.shape[1:], BF16),
            shape(w_down.shape[1:], BF16),
        ),
        in_specs=[VMEM] * 4,
        out_specs=(VMEM, VMEM) + (pl.BlockSpec(memory_space=pltpu.HBM),) * 3,
        scratch_shapes=[pltpu.SemaphoreType.DMA((6 * BLOCKS,))],
        compiler_params=pltpu.CompilerParams(vmem_limit_bytes=24 << 20),
    )(slots, near(incoming), near(mine), near(swap_cores(give)))
    return (grad_tokens, grad_gate[None], grad_up[None], grad_down[None], gate_line[:, :40])


def solution(mesh):
    torus = Mesh(mesh.devices.reshape(8, 2, 2, 4, 4), ("pair", "odd", "core", "x", "y"))
    dp, expert = (*Z, "core"), ("x", "y")
    in_specs = (
        P(expert, dp),
        P(expert, dp),
        P(),
        P(),
        P(expert, dp, None),
        P(expert, dp, None),
        P(expert, None, dp),
    )
    out_specs = (
        P(expert, dp),
        P(expert, dp, None),
        P(expert, dp, None),
        P(expert, None, dp),
        P(expert, None),
    )
    return jax.shard_map(
        per_device, mesh=torus, in_specs=in_specs, out_specs=out_specs, check_vma=False
    )
```

time: 135 us -> 134 us (level)
  waiting for transfers between devices: 10.7 us -> 4.57 us
  starting transfers between devices: 27.4 us -> 30.8 us
  blocking collectives: 88.6 us -> 90.4 us
    ppermute x2, waiting for transfers between devices: 5.79 us -> 0.01 us  [swap_cores(): return lax.ppermute(value, 'core', [(0, 1), (1, 0)])]
    ppermute x2, starting transfers between devices: 15.4 us -> 18.8 us  [swap_cores(): return lax.ppermute(value, 'core', [(0, 1), (1, 0)])]
    pallas_call x1 -> x2, Pallas kernels: 1.54 us -> 4.64 us  [the longest x1 2.68 us: per_device(): pl.pallas_call(last_kernel, out_shape=(shape((TOK, LANES), BF16), shape((...]
    pallas_call x6 -> x4, Pallas kernels: 5.47 us -> 3.02 us  [call(): pl.pallas_call(kernel, out_shape=out_shape, in_specs=[VMEM] * len(inputs)...]
    all_to_all x2, blocking collectives: 24.5 us -> 26.3 us  [the longest x1 14.1 us: per_device(): lax.all_to_all(outgoing, everyone, split_axis=0, concat_axis=0, tiled=True)]
  transfers between devices with their start and end apart: 4 -> 4, of which waited for: 4 -> 2; matrix products, arithmetic and copies ran while one was open for 0% -> 0% of each run, Pallas kernels for 0% -> 0%
where the time goes in v5:
time: 134 us
  blocking collectives  90.4 us (67%)
  starting transfers between devices  30.8 us (23%)
  Pallas kernels  7.66 us (6%)
  waiting for transfers between devices  4.57 us (3%)
    all_gather x1, blocking collectives, per_device(): pieces = lax.all_gather(piece, Z, axis=0, tiled=False)  34.2 us
    all_to_all x1, blocking collectives, per_device(): lax.all_to_all(sums, 'pair', split_axis=0, concat_axis=0, tiled=True)  30 us
    ppermute x2, starting transfers between devices, swap_cores(): return lax.ppermute(value, 'core', [(0, 1), (1, 0)])  18.8 us
    all_to_all x1, blocking collectives, per_device(): lax.all_to_all(outgoing, everyone, split_axis=0, concat_axis=0, tiled=True)  14.1 us
    all_to_all x1, blocking collectives, per_device(): lax.all_to_all(send, everyone, split_axis=0, concat_axis=0, tiled=True)  12.2 us
    ppermute x2, starting transfers between devices, shift(): lax.ppermute(value, Z, [(z, (z + step) % CHIPS) for z in range(CHIPS)])  11.9 us
    ppermute x2, waiting for transfers between devices, shift(): lax.ppermute(value, Z, [(z, (z + step) % CHIPS) for z in range(CHIPS)])  4.57 us
    pallas_call x4, Pallas kernels, call(): pl.pallas_call(kernel, out_shape=out_shape, in_specs=[VMEM] * len(inputs)...  3.02 us
  transfers between devices with their start and end apart: 4, of which 2 were waited for; matrix products, arithmetic and copies ran while one was open for 0% of the time, Pallas kernels for 0%

profile of v5, /device:TPU:1, one launch (start us, length us, event | category | flops | bytes accessed | tf_op | source)
XLA Modules:
  0.0 134.1 jit_solution(550685552824681819)
XLA Ops:
  0.6 2.0 %shard_map.110 = (bf16[32,40,128]{2,1,0:T(8,128)(2,1)S(1)}, s32[4,160]{1,0:T(4,128)S(1)}, f32[4,160]{1,0:T(4,128)S(1)}, bf16[3,8,128,128]{3,2,1,0:T(8,128)(2,1)S(1)}, bf16[3,8,128,128]{3,2,1,0:T(8,128)(2,1)S(1)}) custom-call(s32[4,160]{1,0:T(4,128)} %slots_hbm.1, f32[4,160]{1,0:T(4,128)} %gates_hbm.1, bf16[320,128]{1,0:T(8,128)(2,1)} %tokens_hbm.1, ...), custom_call_target="tpu_custom_call" | custom-call | tf_op jit(solution)/shard_map/pallas_call | solution.py:353
  2.6 8.7 %collective-permute-start = (bf16[3,8,128,128]{3,2,1,0:T(8,128)(2,1)S(1)}, bf16[3,8,128,128]{3,2,1,0:T(8,128)(2,1)S(1)}, u32[]{:S(2)}, u32[]{:S(2)}) collective-permute-start(bf16[3,8,128,128]{3,2,1,0:T(8,128)(2,1)S(1)} %get-tuple-element.29), channel_id=1, source_target_pairs={{0,16},{16,0},{1,17},{17,1},{2,18},{18,2},{3,19},{19,3},{4,20},{20... | collective-permute-start | bytes 2359304 | tf_op jit(solution)/shard_map/ppermute | solution.py:340
  11.4 12.2 %all_to_all.15.recv_ref = bf16[32,40,128]{2,1,0:T(8,128)(2,1)S(1)} all-to-all(bf16[32,40,128]{2,1,0:T(8,128)(2,1)S(1)} %get-tuple-element.27), channel_id=1, replica_groups=mesh['pair'=8,'odd'=2,'core'=2,'x'=4,'y'=4] {'core','x','y'}, dimensions={0} | all-to-all | bytes 655360 | tf_op jit(solution)/shard_map/all_to_all | solution.py:373
  23.6 0.0 collective-permute-done.other_ref
  23.6 1.1 shard_map.111
  24.7 2.4 %collective-permute-start.1 = (bf16[4,240,128]{2,1,0:T(8,128)(2,1)S(1)}, bf16[4,240,128]{2,1,0:T(8,128)(2,1)S(1)}, u32[]{:S(2)}, u32[]{:S(2)}) collective-permute-start(bf16[4,240,128]{2,1,0:T(8,128)(2,1)S(1)} %get-tuple-element.33), channel_id=1, source_target_pairs={{0,32},{32,64},{64,96},{96,128},{128,160},{160,192},{192,224},{224... | collective-permute-start | bytes 737288 | tf_op jit(solution)/shard_map/ppermute | solution.py:348
  27.1 9.5 %collective-permute-start.2 = (bf16[4,240,128]{2,1,0:T(8,128)(2,1)S(1)}, bf16[4,240,128]{2,1,0:T(8,128)(2,1)S(1)}, u32[]{:S(2)}, u32[]{:S(2)}) collective-permute-start(bf16[4,240,128]{2,1,0:T(8,128)(2,1)S(1)} %get-tuple-element.34), channel_id=1, source_target_pairs={{0,480},{32,0},{64,32},{96,64},{128,96},{160,128},{192,160},{224,1... | collective-permute-start | bytes 737288 | tf_op jit(solution)/shard_map/ppermute | solution.py:348
  36.6 3.7 %collective-permute-done.1.from_left_ref = bf16[4,240,128]{2,1,0:T(8,128)(2,1)S(1)} collective-permute-done((bf16[4,240,128]{2,1,0:T(8,128)(2,1)S(1)}, bf16[4,240,128]{2,1,0:T(8,128)(2,1)S(1)}, u32[]{:S(2)}, u32[]{:S(2)}) %collective-permute-start.1) | collective-permute-done | bytes 245792 | tf_op jit(solution)/shard_map/ppermute | solution.py:348
  40.3 0.9 collective-permute-done.2.from_right_ref
  41.2 0.1 shard_map.112
  41.4 30.0 %all_to_all.16.parts_ref = bf16[8,240,128]{2,1,0:T(8,128)(2,1)S(1)} all-to-all(bf16[8,240,128]{2,1,0:T(8,128)(2,1)S(1)} %get-tuple-element.35), channel_id=1, replica_groups=mesh['pair'=8,'odd'=2,'core'=2,'x'=4,'y'=4] {'pair'}, dimensions={0} | all-to-all | bytes 983040 | tf_op jit(solution)/shard_map/all_to_all | solution.py:388
  71.3 0.2 shard_map.113
  71.5 34.2 %all-gather = bf16[3968,128]{1,0:T(8,128)(2,1)S(1)} all-gather(bf16[248,128]{1,0:T(8,128)(2,1)S(1)} %shard_map.113), channel_id=2, replica_groups=mesh['pair'=8,'odd'=2,'core'=2,'x'=4,'y'=4] {'pair','odd'}, dimensions={0}, use_global_device_ids=true | all-gather | bytes 1079296 | tf_op jit(solution)/shard_map/all_gather | solution.py:390
  105.7 1.6 %shard_map.114 = (bf16[3,8,128,128]{3,2,1,0:T(8,128)(2,1)S(1)}, bf16[3,8,128,128]{3,2,1,0:T(8,128)(2,1)S(1)}, f32[32,24,128]{2,1,0:T(8,128)S(1)}) custom-call(s32[4,160]{1,0:T(4,128)S(1)} %get-tuple-element.25.slots_ref, bf16[160,256]{1,0:T(8,128)(2,1)S(1)} %get-tuple-element.30.inputs_ref, bf16[160,256]{1,0:T(8,128)(2,1)S(1)} %get-tuple-element.31.scaled_ref, ...), custom_call_target="tpu_custom_call" | custom-call | tf_op jit(solution)/shard_map/pallas_call | solution.py:318
  107.3 10.1 %collective-permute-start.3 = (bf16[3,8,128,128]{3,2,1,0:T(8,128)(2,1)S(1)}, bf16[3,8,128,128]{3,2,1,0:T(8,128)(2,1)S(1)}, u32[]{:S(2)}, u32[]{:S(2)}) collective-permute-start(bf16[3,8,128,128]{3,2,1,0:T(8,128)(2,1)S(1)} %get-tuple-element.39), channel_id=1, source_target_pairs={{0,16},{16,0},{1,17},{17,1},{2,18},{18,2},{3,19},{19,3},{4,20},{20... | collective-permute-start | bytes 2359304 | tf_op jit(solution)/shard_map/ppermute | solution.py:340
  117.4 14.1 %all_to_all.17.incoming_ref = f32[32,24,128]{2,1,0:T(8,128)S(1)} all-to-all(f32[32,24,128]{2,1,0:T(8,128)S(1)} %get-tuple-element.37), channel_id=1, replica_groups=mesh['pair'=8,'odd'=2,'core'=2,'x'=4,'y'=4] {'core','x','y'}, dimensions={0} | all-to-all | bytes 786432 | tf_op jit(solution)/shard_map/all_to_all | solution.py:396
  131.5 0.0 collective-permute-done.3.other_ref
  131.5 2.7 %shard_map.115 = (bf16[320,128]{1,0:T(8,128)(2,1)}, f32[1,128]{1,0:T(1,128)}, bf16[128,2048]{1,0:T(8,128)(2,1)}, bf16[128,2048]{1,0:T(8,128)(2,1)}, bf16[2048,128]{1,0:T(8,128)(2,1)}) custom-call(s32[4,160]{1,0:T(4,128)S(1)} %get-tuple-element.25.slots_ref, f32[32,24,128]{2,1,0:T(8,128)S(1)} %all_to_all.17.incoming_ref, ...), custom_call_target="tpu_custom_call" | custom-call | tf_op jit(solution)/shard_map/pallas_call | solution.py:397
Async XLA Ops:
  2.6 21.0 %collective-permute-start = (bf16[3,8,128,128]{3,2,1,0:T(8,128)(2,1)S(1)}, bf16[3,8,128,128]{3,2,1,0:T(8,128)(2,1)S(1)}, u32[]{:S(2)}, u32[]{:S(2)}) collective-permute-start(bf16[3,8,128,128]{3,2,1,0:T(8,128)(2,1)S(1)} %get-tuple-element.29), channel_id=1, source_target_pairs={{0,16},{16,0},{1,17},{17,1},{2,18},{18,2},{3,19},{19,3},{4,20},{20... | collective-permute-start | bytes 2359304 | tf_op jit(solution)/shard_map/ppermute | solution.py:340
  24.7 15.6 %collective-permute-start.1 = (bf16[4,240,128]{2,1,0:T(8,128)(2,1)S(1)}, bf16[4,240,128]{2,1,0:T(8,128)(2,1)S(1)}, u32[]{:S(2)}, u32[]{:S(2)}) collective-permute-start(bf16[4,240,128]{2,1,0:T(8,128)(2,1)S(1)} %get-tuple-element.33), channel_id=1, source_target_pairs={{0,32},{32,64},{64,96},{96,128},{128,160},{160,192},{192,224},{224... | collective-permute-start | bytes 737288 | tf_op jit(solution)/shard_map/ppermute | solution.py:348
  27.1 14.1 %collective-permute-start.2 = (bf16[4,240,128]{2,1,0:T(8,128)(2,1)S(1)}, bf16[4,240,128]{2,1,0:T(8,128)(2,1)S(1)}, u32[]{:S(2)}, u32[]{:S(2)}) collective-permute-start(bf16[4,240,128]{2,1,0:T(8,128)(2,1)S(1)} %get-tuple-element.34), channel_id=1, source_target_pairs={{0,480},{32,0},{64,32},{96,64},{128,96},{160,128},{192,160},{224,1... | collective-permute-start | bytes 737288 | tf_op jit(solution)/shard_map/ppermute | solution.py:348
  107.3 24.2 %collective-permute-start.3 = (bf16[3,8,128,128]{3,2,1,0:T(8,128)(2,1)S(1)}, bf16[3,8,128,128]{3,2,1,0:T(8,128)(2,1)S(1)}, u32[]{:S(2)}, u32[]{:S(2)}) collective-permute-start(bf16[3,8,128,128]{3,2,1,0:T(8,128)(2,1)S(1)} %get-tuple-element.39), channel_id=1, source_target_pairs={{0,16},{16,0},{1,17},{17,1},{2,18},{18,2},{3,19},{19,3},{4,20},{20... | collective-permute-start | bytes 2359304 | tf_op jit(solution)/shard_map/ppermute | solution.py:340
